TPU v7x, 256 devices: a whole 4x4x8 slice. The times are simulated.
256 devices in a mesh: slab: 32 (over z_lo, x, core), rep: 8 (over z_hi, y).
Axes of the slice: x: 4, y: 4, z: 8 (z_hi: 2, z_lo: 4; z = z_hi * 4 + z_lo), core: 2. Of those that a mesh axis runs over, the one named last changes fastest.
Arguments:
- features: bfloat16 [8, 96, 64, 4, 256], P('rep', None, 'slab'), may hold values from -6 to 6
- occupancy: int32 [8, 64, 4, 256], P('rep', 'slab'), may hold values from 0 to 1, as said below
- w_fine: bfloat16 [27, 96, 96], replicated, may hold values from -0.125 to 0.125
- w_down: bfloat16 [27, 192, 96], replicated, may hold values from -0.125 to 0.125
- cotangent: bfloat16 [8, 192, 32, 2, 128], P('rep', None, 'slab'), may hold values from -6 to 6
Outputs:
- section_out: bfloat16 [8, 192, 32, 2, 128], P('rep', None, 'slab')
- grad_features: bfloat16 [8, 96, 64, 4, 256], P('rep', None, 'slab')
- grad_fine: float32 [27, 96, 96], replicated
- grad_down: float32 [27, 192, 96], replicated
Inputs may be any that keep to these rules, and one draw needn't show every extreme that they name: `occupancy`: 1 marks an occupied voxel; the share of occupied voxels differs from plane to plane.
All inputs are finite; a program needn't handle non-finite values.
Results may differ from a plain program's by a relative error of at most 0.0058.
Values may be sent and summed in bfloat16 or wider, within the bound.
A program may use at most 128 MiB of HBM per device.

v0:
```python
import jax
import jax.numpy as jnp
from jax import lax
from jax.sharding import PartitionSpec as P


def padded_2(array, sides, width):
    for axis, dim in sides:
        devices, length = (lax.axis_size(axis), array.shape[dim])
        up = [(i, (i + 1) % devices) for i in range(devices - 1)]
        down = [(j, i) for i, j in up]
        last = lax.slice_in_dim(array, length - width, length, axis=dim)
        first = lax.slice_in_dim(array, 0, width, axis=dim)
        before = lax.ppermute(last, axis, up)
        after = lax.ppermute(first, axis, down)
        array = jnp.concatenate([before, array, after], axis=dim)
    return array


def passed_along(array, axis, by):
    devices = lax.axis_size(axis)
    pairs = [(i, i + by) for i in range(devices) if 0 <= i + by < devices]
    return lax.ppermute(array, axis, pairs)


def dsilu(value):
    sig = jax.nn.sigmoid(value)
    return sig * (1.0 + value * (1.0 - sig))


def conv_same(padded, weights):
    planes = padded.shape[1] - 2
    rows = padded.shape[2] - 2
    cols = padded.shape[3] - 2
    total = jnp.zeros((weights.shape[1], planes, rows, cols), jnp.float32)
    for offset in range(27):
        dx, dy, dz = (offset // 9, offset // 3 % 3, offset % 3)
        piece = padded[:, dx : dx + planes, dy : dy + rows, dz : dz + cols]
        total = total + jnp.einsum(
            "dc,cpyz->dpyz", weights[offset], piece, preferred_element_type=jnp.float32
        )
    return total


def wgrad_same(grad, padded):
    planes, rows, cols = (grad.shape[1], grad.shape[2], grad.shape[3])
    parts = []
    for offset in range(27):
        dx, dy, dz = (offset // 9, offset // 3 % 3, offset % 3)
        piece = padded[:, dx : dx + planes, dy : dy + rows, dz : dz + cols]
        parts.append(jnp.einsum("dpyz,cpyz->dc", grad, piece, preferred_element_type=jnp.float32))
    return jnp.stack(parts)


def conv_down(padded, weights):
    planes = (padded.shape[1] - 1) // 2
    rows = (padded.shape[2] - 1) // 2
    cols = (padded.shape[3] - 1) // 2
    total = jnp.zeros((weights.shape[1], planes, rows, cols), jnp.float32)
    for offset in range(27):
        dx, dy, dz = (offset // 9, offset // 3 % 3, offset % 3)
        piece = padded[:, dx : dx + 2 * planes : 2, dy : dy + 2 * rows : 2, dz : dz + 2 * cols : 2]
        total = total + jnp.einsum(
            "dc,cpyz->dpyz", weights[offset], piece, preferred_element_type=jnp.float32
        )
    return total


def wgrad_down(grad, padded):
    planes, rows, cols = (grad.shape[1], grad.shape[2], grad.shape[3])
    parts = []
    for offset in range(27):
        dx, dy, dz = (offset // 9, offset // 3 % 3, offset % 3)
        piece = padded[:, dx : dx + 2 * planes : 2, dy : dy + 2 * rows : 2, dz : dz + 2 * cols : 2]
        parts.append(jnp.einsum("dpyz,cpyz->dc", grad, piece, preferred_element_type=jnp.float32))
    return jnp.stack(parts)


def pad_axis(value, axis, before, after):
    widths = [(0, 0)] * value.ndim
    widths[axis] = (before, after)
    return jnp.pad(value, widths)


def alternate(first, middle, last, axis):
    length = first.shape[axis]
    even = pad_axis(first, axis, 0, 1) + pad_axis(last, axis, 1, 0)
    odd = pad_axis(middle, axis, 0, 1)
    paired = jnp.stack([even, odd], axis=axis + 1)
    shape = list(even.shape)
    shape[axis] = 2 * (length + 1)
    merged = paired.reshape(shape)
    return lax.slice_in_dim(merged, 0, 2 * length + 1, 1, axis)


def back_down(grad, weights):
    terms = [
        jnp.einsum("dc,dpyz->cpyz", weights[offset], grad, preferred_element_type=jnp.float32)
        for offset in range(27)
    ]
    x_lines = []
    for dx in range(3):
        y_lines = []
        for dy in range(3):
            base = 9 * dx + 3 * dy
            y_lines.append(alternate(terms[base], terms[base + 1], terms[base + 2], 3))
        x_lines.append(alternate(y_lines[0], y_lines[1], y_lines[2], 2))
    return alternate(x_lines[0], x_lines[1], x_lines[2], 1)


def local(features, occupancy, w_fine, w_down, cotangent):
    mask = occupancy[0].astype(jnp.float32)
    masked = (features[0] * mask).astype(jnp.bfloat16)
    widened = padded_2(masked, (("slab", 1),), 1)
    fine_pad = jnp.pad(widened, ((0, 0), (0, 0), (1, 1), (1, 1)))
    fine_pre = conv_same(fine_pad, w_fine)
    hidden = (jax.nn.silu(fine_pre) * mask).astype(jnp.bfloat16)
    size_x, size_y, size_z = mask.shape
    coarse_mask = mask.reshape(size_x // 2, 2, size_y // 2, 2, size_z // 2, 2).max(axis=(1, 3, 5))
    below = passed_along(hidden[:, -1:], "slab", 1)
    down_pad = jnp.pad(jnp.concatenate([below, hidden], axis=1), ((0, 0), (0, 0), (1, 0), (1, 0)))
    down_pre = conv_down(down_pad, w_down)
    section_out = (jax.nn.silu(down_pre) * coarse_mask).astype(jnp.bfloat16)
    grad_pre = (cotangent[0] * coarse_mask * dsilu(down_pre)).astype(jnp.bfloat16)
    grad_down = wgrad_down(grad_pre, down_pad)
    spread = back_down(grad_pre, w_down)
    owned = spread[:, 1:, 1:, 1:]
    arriving = passed_along(spread[:, 0, 1:, 1:], "slab", -1)
    grad_hidden = jnp.concatenate([owned[:, :-1], owned[:, -1:] + arriving[:, None]], axis=1)
    grad_fine_pre = (grad_hidden * mask * dsilu(fine_pre)).astype(jnp.bfloat16)
    grad_fine = wgrad_same(grad_fine_pre, fine_pad)
    flipped = jnp.transpose(w_fine[::-1], (0, 2, 1))
    grad_wide = padded_2(grad_fine_pre, (("slab", 1),), 1)
    back_pad = jnp.pad(grad_wide, ((0, 0), (0, 0), (1, 1), (1, 1)))
    grad_features = (conv_same(back_pad, flipped) * mask).astype(jnp.bfloat16)
    total_fine, total_down = lax.psum((grad_fine, grad_down), ("slab", "rep"))
    cell_count = lax.axis_size("rep") * lax.axis_size("slab") * size_x * size_y * size_z // 8
    scale = 1.0 / jnp.sqrt(jnp.float32(cell_count))
    return (section_out[None], grad_features[None], total_fine * scale, total_down * scale)


def solution(mesh):
    return jax.shard_map(
        local,
        mesh=mesh,
        in_specs=(
            P("rep", None, "slab", None, None),
            P("rep", "slab", None, None),
            P(),
            P(),
            P("rep", None, "slab", None, None),
        ),
        out_specs=(
            P("rep", None, "slab", None, None),
            P("rep", None, "slab", None, None),
            P(),
            P(),
        ),
        check_vma=False,
    )
```

profile of v0, /device:TPU:1, one launch (start us, length us, event | category | flops | bytes accessed | tf_op | source)
XLA Modules:
  0.0 519.7 jit_solution(14112734983826789140)
XLA Ops:
  8.0 1.1 fusion.129
  9.2 4.5 collective-permute-start
  13.7 1.9 collective-permute-start.1
  16.9 3.8 collective-permute-done.1
  20.8 1.8 select_maximum_fusion.2
  30.3 1.2 convolution_bitcast_fusion.14
  31.5 1.6 multiply_convert_fusion
  33.9 1.9 collective-permute-start.2
  37.1 1.3 collective-permute-done.2
  38.4 1.4 fusion.127
  39.8 2.6 slice.722
  42.4 2.4 slice.724
  44.8 2.4 slice.726
  47.3 2.4 slice.728
  49.7 2.4 slice.730
  52.1 2.4 slice.732
  54.5 2.5 slice.734
  57.0 2.5 slice.736
  59.5 2.6 slice.738
  62.0 2.4 slice.740
  64.5 2.4 slice.742
  66.9 2.4 slice.744
  69.3 2.4 slice.746
  71.7 2.4 slice.748
  74.1 2.4 slice.750
  76.5 2.7 slice.752
  79.2 2.0 slice.774
  81.2 1.9 slice.772
  83.2 1.9 slice.770
  85.1 1.9 slice.768
  87.0 1.8 slice.766
  88.8 2.4 slice.764
  91.2 2.4 slice.762
  93.7 2.4 slice.760
  96.1 2.4 slice.758
  98.5 2.6 slice.756
  101.1 2.9 slice.754
  104.0 1.1 fusion.348
  156.0 1.1 pad_bitcast_fusion.11
  157.4 1.1 pad_bitcast_fusion.10
  161.6 1.7 slice.878
  163.3 1.1 pad_bitcast_fusion.8
  165.3 1.7 slice.879
  167.0 1.1 pad_bitcast_fusion.7
  170.1 1.3 add_bitcast_fusion.2
  173.8 1.7 slice.882
  175.4 1.1 pad_bitcast_fusion.5
  177.5 1.7 slice.883
  179.2 1.1 pad_bitcast_fusion.4
  182.3 1.3 add_bitcast_fusion.1
  185.1 1.7 pad_maximum_fusion
  186.8 3.6 copy.123
  190.4 1.6 fusion.467
  192.0 2.1 collective-permute-start.3
  196.5 5.5 %collective-permute-done.3 = f32[96,4,256]{2,0,1:T(8,128)S(1)} collective-permute-done((f32[96,4,256]{2,0,1:T(8,128)S(1)}, f32[96,4,256]{2,0,1:T(8,128)S(1)}, u32[]{:S(2)}, u32[]{:S(2)}) %collective-permute-start.3) | collective-permute-done | bytes 393248 | tf_op jit(solution)/shard_map/ppermute | solution.py:23
  202.0 1.2 slice_add_fusion
  224.0 1.8 fusion.104
  229.6 1.9 collective-permute-start.4
  231.5 2.8 collective-permute-start.5
  234.6 4.1 collective-permute-done.5
  248.1 1.1 copy.126
  249.2 258.6 %all-reduce.45.cloned.1.call-done = (f32[27,96,96]{2,1,0:T(8,128)}, f32[27,192,96]{2,1,0:T(8,128)}) async-done(((f32[27,96,96]{2,1,0:T(8,128)}, f32[27,192,96]{2,1,0:T(8,128)}), (f32[27,96,96]{2,1,0:T(8,128)}, f32[27,192,96]{2,1,0:T(8,128)})) %all-reduce.45.cloned.1.call-update) | async-done | bytes 2986000 | tf_op jit(solution)/shard_map/psum | solution.py:136
  507.8 3.6 broadcast_multiply_fusion
  511.4 1.2 broadcast_multiply_fusion.1
  (307 shorter events, 111.8 us)
Async XLA Ops:
  7.2 8.8 %copy-start.9 = (bf16[1,96,2,4,256]{4,3,2,1,0:T(4,128)(2,1)S(1)}, bf16[1,96,2,4,256]{4,3,2,1,0:T(4,128)(2,1)}, u32[]{:S(2)}) copy-start(bf16[1,96,2,4,256]{4,3,2,1,0:T(4,128)(2,1)} %param.5) | copy-start | bytes 1179652
  7.2 8.4 %copy-start.3 = (bf16[27,96,96]{2,1,0:T(8,128)(2,1)S(1)}, bf16[27,96,96]{2,1,0:T(8,128)(2,1)}, u32[]{:S(2)}) copy-start(bf16[27,96,96]{2,1,0:T(8,128)(2,1)} %param.7) | copy-start | bytes 1492996
  7.2 500.6 %all-reduce.45.cloned.1.call-start = ((), (), s32[]{:S(2)}) async-start(), calls=%async_computation | async-start | bytes 7962624 | tf_op jit(solution)/shard_map/psum | solution.py:136
  8.0 23.5 %copy-start.42 = (f32[2,4,256]{2,1,0:T(4,128)}, f32[2,4,256]{2,1,0:T(4,128)S(1)}, u32[]{:S(2)}) copy-start(f32[2,4,256]{2,1,0:T(4,128)S(1)} %convert_bitcast_fusion.1) | copy-start | bytes 24580
  9.2 7.1 %collective-permute-start = (bf16[96,1,4,256]{3,0,2,1:T(8,128)(2,1)S(1)}, bf16[96,1,4,256]{3,0,2,1:T(8,128)(2,1)S(1)}, u32[]{:S(2)}, u32[]{:S(2)}) collective-permute-start(bf16[96,1,4,256]{3,0,2,1:T(8,128)(2,1)S(1)} %get-tuple-element.22), channel_id=1, source_target_pairs={{0,8},{8,16},{16,24},{24,32},{32,40},{40,48},{48,56},{56,64},{64,7... | collective-permute-start | bytes 589832 | tf_op jit(solution)/shard_map/ppermute | solution.py:14
  13.7 7.1 %collective-permute-start.1 = (bf16[96,1,4,256]{3,0,2,1:T(8,128)(2,1)S(1)}, bf16[96,1,4,256]{3,0,2,1:T(8,128)(2,1)}, u32[]{:S(2)}, u32[]{:S(2)}) collective-permute-start(bf16[96,1,4,256]{3,0,2,1:T(8,128)(2,1)S(1)} %get-tuple-element.23), channel_id=1, source_target_pairs={{8,0},{16,8},{24,16},{32,24},{40,32},{48,40},{56,48},{64,56},{72,6... | collective-permute-start | bytes 589832 | tf_op jit(solution)/shard_map/ppermute | solution.py:15
  16.3 0.7 copy-start.6
  28.5 0.9 copy-start.7
  31.5 4.3 copy-start.45
  33.1 0.7 copy-start.5
  33.9 4.5 collective-permute-start.2
  103.9 6.0 %copy-start = (bf16[27,192,96]{2,1,0:T(8,128)(2,1)S(1)}, bf16[27,192,96]{2,1,0:T(8,128)(2,1)}, u32[]{:S(2)}) copy-start(bf16[27,192,96]{2,1,0:T(8,128)(2,1)} %param.8) | copy-start | bytes 2985988
  103.9 6.0 %copy-start.11 = (bf16[96,1,2,128]{3,0,2,1:T(8,128)(2,1)S(1)}, bf16[96,1,2,128]{3,0,2,1:T(8,128)(2,1)}, u32[]{:S(2)}) copy-start(bf16[96,1,2,128]{3,0,2,1:T(8,128)(2,1)} %slice.764) | copy-start | bytes 147460
  104.0 6.1 %copy-start.12 = (bf16[96,1,2,128]{3,0,2,1:T(8,128)(2,1)S(1)}, bf16[96,1,2,128]{3,0,2,1:T(8,128)(2,1)}, u32[]{:S(2)}) copy-start(bf16[96,1,2,128]{3,0,2,1:T(8,128)(2,1)} %slice.762) | copy-start | bytes 147460
  104.0 6.3 %copy-start.13 = (bf16[96,1,2,128]{3,0,2,1:T(8,128)(2,1)S(1)}, bf16[96,1,2,128]{3,0,2,1:T(8,128)(2,1)}, u32[]{:S(2)}) copy-start(bf16[96,1,2,128]{3,0,2,1:T(8,128)(2,1)} %slice.760) | copy-start | bytes 147460
  104.0 6.4 %copy-start.14 = (bf16[96,1,2,128]{3,0,2,1:T(8,128)(2,1)S(1)}, bf16[96,1,2,128]{3,0,2,1:T(8,128)(2,1)}, u32[]{:S(2)}) copy-start(bf16[96,1,2,128]{3,0,2,1:T(8,128)(2,1)} %slice.758) | copy-start | bytes 147460
  104.0 6.6 %copy-start.15 = (bf16[96,1,2,128]{3,0,2,1:T(8,128)(2,1)S(1)}, bf16[96,1,2,128]{3,0,2,1:T(8,128)(2,1)}, u32[]{:S(2)}) copy-start(bf16[96,1,2,128]{3,0,2,1:T(8,128)(2,1)} %slice.756) | copy-start | bytes 147460
  104.0 6.8 %copy-start.32 = (bf16[96,1,2,128]{3,0,2,1:T(8,128)(2,1)S(1)}, bf16[96,1,2,128]{3,0,2,1:T(8,128)(2,1)}, u32[]{:S(2)}) copy-start(bf16[96,1,2,128]{3,0,2,1:T(8,128)(2,1)} %slice.724) | copy-start | bytes 147460
  105.1 5.9 %copy-start.31 = (bf16[96,1,2,128]{3,0,2,1:T(8,128)(2,1)S(1)}, bf16[96,1,2,128]{3,0,2,1:T(8,128)(2,1)}, u32[]{:S(2)}) copy-start(bf16[96,1,2,128]{3,0,2,1:T(8,128)(2,1)} %slice.726) | copy-start | bytes 147460
  106.1 5.1 copy-start.30
  108.0 3.3 copy-start.29
  109.9 1.5 copy-start.28
  110.1 1.6 copy-start.27
  110.4 1.4 copy-start.26
  110.8 1.2 copy-start.25
  110.9 1.2 copy-start.24
  111.1 1.3 copy-start.23
  111.3 1.3 copy-start.21
  111.5 1.2 copy-start.20
  111.7 1.2 copy-start.19
  111.8 1.2 copy-start.18
  112.0 1.2 copy-start.17
  112.2 1.2 copy-start.22
  112.2 1.2 copy-start.44
  113.1 1.3 copy-start.16
  159.5 0.9 copy-start.39
  159.5 0.9 copy-start.40
  159.5 1.0 copy-start.41
  160.7 6.4 %copy-start.38 = (f32[96,1,2,128]{3,0,2,1:T(8,128)S(1)}, f32[96,1,2,128]{3,0,2,1:T(8,128)}, u32[]{:S(2)}) copy-start(f32[96,1,2,128]{3,0,2,1:T(8,128)} %convolution_bitcast_fusion.66) | copy-start | bytes 294916
  171.7 1.0 copy-start.35
  171.7 1.0 copy-start.36
  171.7 1.0 copy-start.37
  172.9 6.3 %copy-start.34 = (f32[96,1,2,128]{3,0,2,1:T(8,128)S(1)}, f32[96,1,2,128]{3,0,2,1:T(8,128)}, u32[]{:S(2)}) copy-start(f32[96,1,2,128]{3,0,2,1:T(8,128)} %convolution_bitcast_fusion.57) | copy-start | bytes 294916
  183.9 1.1 copy-start.2
  186.8 7.3 %copy-start.33 = (bf16[1,192,1,2,128]{4,1,3,2,0:T(8,128)(2,1)S(1)}, bf16[1,192,1,2,128]{4,1,3,2,0:T(8,128)(2,1)}, u32[]{:S(2)}) copy-start(bf16[1,192,1,2,128]{4,1,3,2,0:T(8,128)(2,1)} %get-tuple-element.25) | copy-start | bytes 294916
  190.4 12.8 %copy-start.1 = (f32[96,2,4,256]{3,0,2,1:T(8,128)S(1)}, f32[96,2,4,256]{3,0,2,1:T(8,128)}, u32[]{:S(2)}) copy-start(f32[96,2,4,256]{3,0,2,1:T(8,128)} %get-tuple-element.27) | copy-start | bytes 2359300
  190.4 12.8 %copy-start.43 = (f32[2,4,256]{2,1,0:T(4,128)S(1)}, f32[2,4,256]{2,1,0:T(4,128)}, u32[]{:S(2)}) copy-start(f32[2,4,256]{2,1,0:T(4,128)} %copy-done.42) | copy-start | bytes 24580
  192.0 9.9 %collective-permute-start.3 = (f32[96,4,256]{2,0,1:T(8,128)S(1)}, f32[96,4,256]{2,0,1:T(8,128)S(1)}, u32[]{:S(2)}, u32[]{:S(2)}) collective-permute-start(f32[96,4,256]{2,0,1:T(8,128)S(1)} %get-tuple-element.19), channel_id=1, source_target_pairs={{8,0},{16,8},{24,16},{32,24},{40,32},{48,40},{56,48},{64,56},{72,6... | collective-permute-start | bytes 1179656 | tf_op jit(solution)/shard_map/ppermute | solution.py:23
  204.4 2.9 copy-start.8
  229.6 5.0 collective-permute-start.4
  231.5 2.8 copy-start.4
  231.5 7.1 %collective-permute-start.5 = (bf16[96,1,4,256]{3,0,2,1:T(8,128)(2,1)S(1)}, bf16[96,1,4,256]{3,0,2,1:T(8,128)(2,1)S(1)}, u32[]{:S(2)}, u32[]{:S(2)}) collective-permute-start(bf16[96,1,4,256]{3,0,2,1:T(8,128)(2,1)S(1)} %get-tuple-element.21), channel_id=1, source_target_pairs={{8,0},{16,8},{24,16},{32,24},{40,32},{48,40},{56,48},{64,56},{72,6... | collective-permute-start | bytes 589832 | tf_op jit(solution)/shard_map/ppermute | solution.py:15
  507.8 3.6 copy-start.10
Sparse Core Ops, SparseCore 0:
  234.4 273.3 all-reduce.44
where the time goes:
time: 528 us; the launch traced here: 520 us
  waiting for transfers between devices  273 us (52%)
  matrix products  98 us (19%)
  local copies, waits for them, and re-layouts  92.5 us (18%)
  other arithmetic  25 us (5%)
  between operations  15.6 us (3%)
  starting transfers between devices  15.2 us (3%)
    psum x1, waiting for transfers between devices, local(): total_fine, total_down = lax.psum((grad_fine, grad_down), ('slab', 'rep'))  259 us
    slice x27, local copies, waits for them, and re-layouts, conv_down(): padded[:, dx:dx + 2 * planes:2, dy:dy + 2 * rows:2, dz:dz + 2 * cols:2]  64 us
    dot_general x27, matrix products, wgrad_same(): jnp.einsum('dpyz,cpyz->dc', grad, piece, preferred_element_type=jnp.float32)  26 us
    dot_general x27, matrix products, wgrad_down(): jnp.einsum('dpyz,cpyz->dc', grad, piece, preferred_element_type=jnp.float32)  21.9 us
    dot_general x27, matrix products, back_down(): jnp.einsum('dc,dpyz->cpyz', weights[offset], grad, preferred_element_type...  20.9 us
    dot_general x54, matrix products, conv_same(): jnp.einsum('dc,cpyz->dpyz', weights[offset], piece, preferred_element_typ...  19.4 us
    another operation x26, other arithmetic, alternate(): paired = jnp.stack([even, odd], axis=axis + 1)  12.6 us
  transfers between devices with their start and end apart: 7, of which 5 were waited for; matrix products, arithmetic and copies ran while one was open for 3% of the time, Pallas kernels for 0%

commit v1 on v0

v1 whole, which is shorter than its diff:
```python
import jax
import jax.numpy as jnp
from jax import lax
from jax.experimental import pallas as pl
from jax.experimental.pallas import tpu as pltpu
from jax.sharding import PartitionSpec as P

BF = jnp.bfloat16
F32 = jnp.float32
NT = (((1,), (1,)), ((), ()))
HD = 176
HF = 96


def mm(a, b):
    return jnp.dot(a, b, preferred_element_type=F32)


def mm_nt(a, b):
    return lax.dot_general(a, b, NT, preferred_element_type=F32)


def lane_ids(shape):
    return lax.broadcasted_iota(jnp.int32, shape, 1)


def from_before(v):
    return jnp.where(lane_ids(v.shape) == 0, 0.0, pltpu.roll(v, 1, 1))


def from_after(v):
    n = v.shape[1]
    return jnp.where(lane_ids(v.shape) == n - 1, 0.0, pltpu.roll(v, n - 1, 1))


def split_z(n):
    r = lax.broadcasted_iota(jnp.int32, (n, n), 0)
    c = lax.broadcasted_iota(jnp.int32, (n, n), 1)
    src = jnp.where(c < n // 2, 2 * c, 2 * c - n + 1)
    return (r == src).astype(F32).astype(BF)


def join_z(n):
    r = lax.broadcasted_iota(jnp.int32, (n, n), 0)
    c = lax.broadcasted_iota(jnp.int32, (n, n), 1)
    src = jnp.where(r < n // 2, 2 * r, 2 * r - n + 1)
    return (c == src).astype(F32).astype(BF)


def gather_dz(acc, c):
    a0, a1, a2 = acc[:c], acc[c : 2 * c], acc[2 * c :]
    even = from_before(a0[:, 128:]) + a1[:, :128] + a2[:, 128:]
    odd = a0[:, :128] + a1[:, 128:] + from_after(a2[:, :128])
    return jnp.concatenate([even, odd], axis=1)


class Place:
    def __init__(self):
        self.slab = lax.axis_index("slab")
        self.rep = lax.axis_index("rep")
        self.core = self.slab % 2
        self.x = (self.slab // 2) % 4
        self.zlo = self.slab // 8
        self.y = self.rep % 4
        self.zhi = self.rep // 4
        self.z = self.zhi * 4 + self.zlo

    def at(self, core, x, y, z):
        return {"slab": (z % 4) * 8 + x * 2 + core, "rep": (z // 4) * 4 + y}

    def partner(self):
        return self.at(1 - self.core, self.x, self.y, self.z)

    def plane(self, k, sign=1):
        x = (self.x + sign * (k // 4) + 4) % 4
        y = (self.y + sign * (k % 4) + 4) % 4
        return x, y

    def plane_dev(self, k):
        x, y = self.plane(k)
        return self.at(self.core, x, y, self.z)

    def z_dev(self, k):
        return self.at(self.core, self.x, self.y, (self.z + k) % 8)


def remote(src, dst, ssem, rsem, dev):
    return pltpu.make_async_remote_copy(
        src_ref=src, dst_ref=dst, send_sem=ssem, recv_sem=rsem, device_id=dev,
        device_id_type=pl.DeviceIdType.MESH,
    )


class Sum:
    def __init__(self, at, h, part, out, cbuf, acc, rs, zb, sems):
        self.at, self.h = at, h
        self.part, self.out, self.cbuf, self.acc, self.rs, self.zb = part, out, cbuf, acc, rs, zb
        self.ss, self.rr = sems
        self.sent = []

    def rows(self, start):
        return pl.ds(pl.multiple_of(start, 16), self.h)

    def copy(self, src, dst, i, dev):
        c = remote(src, dst, self.ss.at[i], self.rr.at[i], dev)
        c.start()
        self.sent.append(c)
        return c

    def half(self, core):
        return pl.ds(pl.multiple_of(core * (16 * self.h), 16), 16 * self.h)

    def one(self):
        self.c1 = self.copy(self.part.at[self.half(1 - self.at.core)], self.cbuf, 0, self.at.partner())

    def two(self):
        self.c1.wait_recv()
        h, at = self.h, self.at
        self.c2 = []
        for k in list(range(1, 16)) + [0]:
            x, y = at.plane(k)
            m = x * 4 + y
            mine = self.part[self.rows(at.core * (16 * h) + m * h), :].astype(F32)
            both = mine + self.cbuf[self.rows(m * h), :].astype(F32)
            self.acc[self.rows(m * h), :] = both.astype(BF)
            if k:
                self.c2.append(self.copy(self.acc.at[self.rows(m * h)], self.rs.at[k], k, at.plane_dev(k)))

    def three(self):
        h, at = self.h, self.at
        total = self.acc[self.rows((at.x * 4 + at.y) * h), :].astype(F32)
        for k in range(1, 16):
            self.c2[k - 1].wait_recv()
            total = total + self.rs[k].astype(F32)
        self.zb[at.z] = total.astype(BF)
        self.c3 = [
            self.copy(self.zb.at[at.z], self.zb.at[at.z], 16 + k, at.z_dev(k)) for k in range(1, 8)
        ]

    def four(self):
        h, at = self.h, self.at
        for c in self.c3:
            c.wait_recv()
        total = self.zb[0].astype(F32)
        for k in range(1, 8):
            total = total + self.zb[k].astype(F32)
        mine = self.rows(at.core * (16 * h) + (at.x * 4 + at.y) * h)
        self.out[mine, :] = total.astype(BF)
        self.c4 = [
            self.copy(self.out.at[mine], self.out.at[mine], 24 + k, at.plane_dev(k)) for k in range(1, 16)
        ]
        self.c5 = [self.copy(self.out.at[mine], self.out.at[mine], 40, at.partner())]

    def five(self):
        h, at = self.h, self.at
        for k in range(1, 16):
            self.c4[k - 1].wait_recv()
            x, y = at.plane(k, -1)
            rows = self.rows(at.core * (16 * h) + (x * 4 + y) * h)
            self.c5.append(self.copy(self.out.at[rows], self.out.at[rows], 40 + k, at.partner()))

    def six(self):
        for c in self.c5:
            c.wait_recv()
        for c in self.sent:
            c.wait_send()


def kernel(
    xm, occ, wf, wft, wd, wdt, cot,
    gf, so, dout, fout,
    xb, gb, hb, hs, ds, kf, kb, kd, gs, gp, gn, raw,
    dpart, dcb, dacc, drs, dzb, fpart, fcb, facc, frs, fzb,
    hs_s, hs_r, dsem_s, dsem_r, fsem_s, fsem_r,
):
    at = Place()
    first, last = at.slab == 0, at.slab == 31
    left = {"slab": jnp.maximum(at.slab - 1, 0), "rep": at.rep}
    right = {"slab": jnp.minimum(at.slab + 1, 31), "rep": at.rep}
    barrier = pltpu.get_barrier_semaphore()

    def greet(dev):
        pl.semaphore_signal(barrier, 1, device_id=dev, device_id_type=pl.DeviceIdType.MESH)

    @pl.when(jnp.logical_not(first))
    def _():
        greet(left)

    @pl.when(jnp.logical_not(last))
    def _():
        greet(right)

    for k in range(1, 16):
        greet(at.plane_dev(k))
    for k in range(1, 8):
        greet(at.z_dev(k))

    kf[...] = jnp.zeros_like(kf)
    kb[...] = jnp.zeros_like(kb)
    kd[...] = jnp.zeros_like(kd)
    for j in range(9):
        kf[:, 128 * j : 128 * j + 96] = wf[3 * j : 3 * j + 3].reshape(288, 96)
        kb[:, 128 * j : 128 * j + 96] = wft[3 * j : 3 * j + 3].reshape(288, 96)
    for o in range(27):
        kd[:, 128 * o : 128 * o + 96] = wd[o]

    pz = split_z(256)
    for b in (xb, gb):
        for p in range(4):
            b[p, 0] = jnp.zeros((128, 256), BF)
            b[p, 5] = jnp.zeros((128, 256), BF)
            for q in range(1, 5):
                b[p, q, 96:] = jnp.zeros((32, 256), BF)
    for p in range(3):
        hb[p, 0] = jnp.zeros((96, 256), BF)
    for o in range(27):
        hs[128 * o + 96 : 128 * o + 128, :] = jnp.zeros((32, 256), BF)

    amount = 22 + jnp.where(first, 0, 1) + jnp.where(last, 0, 1)
    pl.semaphore_wait(barrier, amount)

    def exchange(src_l, dst_l, src_r, dst_r, i, zero_l, zero_r):
        cl = remote(src_l, dst_l, hs_s.at[i], hs_r.at[i], left) if src_l is not None else None
        cr = remote(src_r, dst_r, hs_s.at[i + 1], hs_r.at[i + 1], right) if src_r is not None else None

        def start():
            if cl is not None:
                @pl.when(jnp.logical_not(first))
                def _():
                    cl.start()
            if cr is not None:
                @pl.when(jnp.logical_not(last))
                def _():
                    cr.start()

        def arrive():
            if cl is not None:
                @pl.when(jnp.logical_not(last))
                def _():
                    cl.wait_recv()

                @pl.when(last)
                def _():
                    zero_l()
            if cr is not None:
                @pl.when(jnp.logical_not(first))
                def _():
                    cr.wait_recv()

                @pl.when(first)
                def _():
                    zero_r()

        def done():
            if cl is not None:
                @pl.when(jnp.logical_not(first))
                def _():
                    cl.wait_send()
            if cr is not None:
                @pl.when(jnp.logical_not(last))
                def _():
                    cr.wait_send()

        return start, arrive, done

    def fill(ref):
        def f():
            ref[...] = jnp.zeros(ref.shape, BF)
        return f

    a_start, a_arrive, a_done = exchange(
        xm.at[0], raw.at[1], xm.at[1], raw.at[0], 0, fill(raw.at[1]), fill(raw.at[0])
    )
    a_start()
    masks = []
    for p in range(2):
        masks.append(mm(occ[p].astype(F32).astype(BF), pz))
    mask = lambda p, q: masks[p][q : q + 1]
    for p in range(2):
        for q in range(4):
            xb[1 + p, 1 + q, :96] = mm(xm[p, q], pz).astype(BF)
    a_arrive()
    for p in range(2):
        for q in range(4):
            xb[3 * p, 1 + q, :96] = mm(raw[p, q], pz).astype(BF)

    b_start, b_arrive, b_done = exchange(
        None, None, hb.at[2, pl.ds(1, 4)], hb.at[0, pl.ds(1, 4)], 2, None, fill(hb.at[0, pl.ds(1, 4)])
    )

    def conv(weights, b, p, q):
        stack = jnp.concatenate([b[p + dx, q + dy] for dx in range(3) for dy in range(3)], axis=0)
        return gather_dz(mm(weights[...], stack), 96)

    for p in (1, 0):
        for q in range(4):
            pre = conv(kf, xb, p, q)
            sig = jax.nn.sigmoid(pre)
            hb[1 + p, 1 + q] = (pre * sig * mask(p, q)).astype(BF)
            ds[p, q] = mask(p, q) * (sig * (1.0 + pre * (1.0 - sig)))
        if p == 1:
            b_start()

    def fill_hs(dx):
        for dy in range(3):
            for j in range(2):
                v = hb[dx, 2 * j + dy]
                lanes = slice(128 * j, 128 * j + 128)
                base = 128 * (9 * dx + 3 * dy)
                hs[base : base + 96, lanes] = from_before(v[:, 128:].astype(F32)).astype(BF)
                hs[base + 128 : base + 224, lanes] = v[:, :128]
                hs[base + 256 : base + 352, lanes] = v[:, 128:]

    fill_hs(1)
    fill_hs(2)
    b_arrive()
    fill_hs(0)
    down = mm(kd[...], hs[...])
    coarse = []
    for j in range(2):
        m = [mask(p, 2 * j + q) for p in range(2) for q in range(2)]
        m = jnp.maximum(jnp.maximum(m[0], m[1]), jnp.maximum(m[2], m[3]))
        coarse.append(jnp.maximum(m[:, :128], m[:, 128:]))
    cm = jnp.concatenate(coarse, axis=1)
    sig = jax.nn.sigmoid(down)
    so[...] = (down * sig * cm).astype(BF)
    gp[...] = (cot[...].astype(F32) * cm * (sig * (1.0 + down * (1.0 - sig)))).astype(BF)
    c_start, c_arrive, c_done = exchange(gp, gn, None, None, 4, fill(gn), None)
    c_start()

    dsum = Sum(at, HD, dpart, dout, dcb, dacc, drs, dzb, (dsem_s, dsem_r))
    fsum = Sum(at, HF, fpart, fout, fcb, facc, frs, fzb, (fsem_s, fsem_r))
    for o in range(27):
        dpart[192 * o : 192 * o + 192, :] = mm_nt(gp[...], hs[128 * o : 128 * o + 128, :]).astype(BF)
    dpart[27 * 192 :, :] = jnp.zeros((32 * HD - 27 * 192, 128), BF)
    dsum.one()

    def back(dx, g):
        r = mm(wdt[9 * dx : 9 * dx + 9].reshape(864, 192), g[...])
        out = []
        for q, terms in enumerate((((0, 1),), ((0, 2), (1, 0)), ((1, 1),), ((1, 2),))):
            even, odd = 0.0, 0.0
            for j, dy in terms:
                lanes = slice(128 * j, 128 * j + 128)
                r0, r1, r2 = [r[96 * (3 * dy + dz) : 96 * (3 * dy + dz) + 96, lanes] for dz in range(3)]
                even = even + r1
                odd = odd + r2 + from_after(r0)
            out.append(jnp.concatenate([even, odd], axis=1))
        return out

    for q, v in enumerate(back(1, gp)):
        gb[1, 1 + q, :96] = (v * ds[0, q]).astype(BF)
    own = back(2, gp)
    c_arrive()
    nxt = back(0, gn)
    for q in range(4):
        gb[2, 1 + q, :96] = ((own[q] + nxt[q]) * ds[1, q]).astype(BF)
    inner = (pl.ds(1, 4), pl.ds(0, 96))
    d_start, d_arrive, d_done = exchange(
        gb.at[(1,) + inner], gb.at[(3,) + inner], gb.at[(2,) + inner], gb.at[(0,) + inner], 6,
        fill(gb.at[(3,) + inner]), fill(gb.at[(0,) + inner]),
    )
    d_start()
    dsum.two()

    for p in range(2):
        for q in range(4):
            g = gb[1 + p, 1 + q, :96].astype(F32)
            ge, go = g[:, :128], g[:, 128:]
            base = 256 * (4 * p + q)
            gs[0:96, base : base + 128] = go.astype(BF)
            gs[0:96, base + 128 : base + 256] = from_after(ge).astype(BF)
            gs[96:192, base : base + 256] = g.astype(BF)
            gs[192:288, base : base + 128] = from_before(go).astype(BF)
            gs[192:288, base + 128 : base + 256] = ge.astype(BF)
    for j0 in range(0, 9, 2):
        js = [j for j in (j0, j0 + 1) if j < 9]
        rhs = jnp.concatenate(
            [
                jnp.concatenate([xb[p + j // 3, q + j % 3] for p in range(2) for q in range(4)], axis=1)
                for j in js
            ],
            axis=0,
        )
        r = mm_nt(gs[...], rhs)
        for i, j in enumerate(js):
            fpart[288 * j : 288 * j + 288, :] = r[:, 128 * i : 128 * i + 128].astype(BF)
    fpart[27 * 96 :, :] = jnp.zeros((32 * HF - 27 * 96, 128), BF)
    fsum.one()
    dsum.three()
    fsum.two()
    d_arrive()

    jz = join_z(256)
    for p in range(2):
        for q in range(4):
            g = (conv(kb, gb, p, q) * mask(p, q)).astype(BF)
            gf[p, q] = mm(g, jz).astype(BF)
    dsum.four()
    fsum.three()
    dsum.five()
    fsum.four()
    fsum.five()
    dsum.six()
    fsum.six()
    a_done()
    b_done()
    c_done()
    d_done()


def local(features, occupancy, w_fine, w_down, cotangent):
    mask = occupancy[0].astype(F32)
    masked = (features[0] * mask).astype(BF)
    xm = jnp.transpose(masked, (1, 2, 0, 3))
    wft = jnp.transpose(w_fine[::-1], (0, 2, 1))
    wdt = jnp.transpose(w_down, (0, 2, 1))
    cot = cotangent[0].reshape(192, 256)
    vm = pl.BlockSpec(memory_space=pltpu.VMEM)

    def sums(h):
        return [
            pltpu.VMEM((32 * h, 128), BF), pltpu.VMEM((16 * h, 128), BF), pltpu.VMEM((16 * h, 128), BF),
            pltpu.VMEM((16, h, 128), BF), pltpu.VMEM((8, h, 128), BF),
        ]

    dma = pltpu.SemaphoreType.DMA
    gf, so, dout, fout = pl.pallas_call(
        kernel,
        out_shape=(
            jax.ShapeDtypeStruct((2, 4, 96, 256), BF),
            jax.ShapeDtypeStruct((192, 256), BF),
            jax.ShapeDtypeStruct((32 * HD, 128), BF),
            jax.ShapeDtypeStruct((32 * HF, 128), BF),
        ),
        in_specs=[vm] * 7,
        out_specs=(vm,) * 4,
        scratch_shapes=[
            pltpu.VMEM((4, 6, 128, 256), BF),
            pltpu.VMEM((4, 6, 128, 256), BF),
            pltpu.VMEM((3, 5, 96, 256), BF),
            pltpu.VMEM((27 * 128, 256), BF),
            pltpu.VMEM((2, 4, 96, 256), F32),
            pltpu.VMEM((288, 1152), BF),
            pltpu.VMEM((288, 1152), BF),
            pltpu.VMEM((192, 27 * 128), BF),
            pltpu.VMEM((288, 2048), BF),
            pltpu.VMEM((192, 256), BF),
            pltpu.VMEM((192, 256), BF),
            pltpu.VMEM((2, 4, 96, 256), BF),
        ]
        + sums(HD)
        + sums(HF)
        + [dma((8,)), dma((8,)), dma((56,)), dma((56,)), dma((56,)), dma((56,))],
        compiler_params=pltpu.CompilerParams(
            collective_id=0, has_side_effects=True, vmem_limit_bytes=60 * 2**20
        ),
        name="section",
    )(xm, occupancy[0], w_fine, wft, w_down, wdt, cot)
    scale = 1.0 / jnp.sqrt(jnp.float32(65536))
    total_down = dout[: 27 * 192].reshape(27, 192, 128)[:, :, :96].astype(F32) * scale
    total_fine = fout[: 27 * 96].reshape(27, 96, 128)[:, :, :96].astype(F32) * scale
    return (
        so.reshape(1, 192, 1, 2, 128),
        jnp.transpose(gf, (2, 0, 1, 3))[None],
        total_fine,
        total_down,
    )


def solution(mesh):
    return jax.shard_map(
        local,
        mesh=mesh,
        in_specs=(
            P("rep", None, "slab", None, None),
            P("rep", "slab", None, None),
            P(),
            P(),
            P("rep", None, "slab", None, None),
        ),
        out_specs=(
            P("rep", None, "slab", None, None),
            P("rep", None, "slab", None, None),
            P(),
            P(),
        ),
        check_vma=False,
    )
```

time: 528 us -> 88.6 us (0.17); the launches traced: 520 us -> 88.4 us
  waiting for transfers between devices: 273 us -> 0 us
  matrix products: 98 us -> 0 us
  local copies, waits for them, and re-layouts: 92.5 us -> 7.69 us
  Pallas kernels: 0 us -> 76.2 us
  other arithmetic: 25 us -> 3.87 us
  starting transfers between devices: 15.2 us -> 0 us
  between operations: 15.6 us -> 0.7 us
    psum x1 -> x0, waiting for transfers between devices: 259 us -> none  [local(): total_fine, total_down = lax.psum((grad_fine, grad_down), ('slab', 'rep'))]
    dot_general x162 -> x0, matrix products: 98 us -> none  [the longest x27 26 us: wgrad_same(): jnp.einsum('dpyz,cpyz->dc', grad, piece, preferred_element_type=jnp.float32)]
    pallas_call x0 -> x1, Pallas kernels: none -> 76.2 us  [local(): pl.pallas_call(kernel, out_shape=(jax.ShapeDtypeStruct((2, 4, 96, 256), B...]
    slice x43 -> x2, local copies, waits for them, and re-layouts: 75.4 us -> 1.45 us  [the longest x1 1.41 us: local(): dout[:27 * 192].reshape(27, 192, 128)[:, :, :96].astype(F32) * scale]
    ppermute x6 -> x0, starting transfers between devices: 15.1 us -> none  [the longest x2 6.42 us: padded_2(): before = lax.ppermute(last, axis, up)]
    ppermute x6 -> x0, waiting for transfers between devices: 14.7 us -> none  [the longest x2 7.88 us: padded_2(): after = lax.ppermute(first, axis, down)]
    another operation x26 -> x0, other arithmetic: 12.6 us -> none  [alternate(): paired = jnp.stack([even, odd], axis=axis + 1)]
    another operation x17 -> x0, local copies, waits for them, and re-layouts: 10.5 us -> none  [alternate(): paired = jnp.stack([even, odd], axis=axis + 1)]
  transfers between devices with their start and end apart: 7 -> 0, of which waited for: 5 -> 0; matrix products, arithmetic and copies ran while one was open for 3% -> 0% of each run, Pallas kernels for 0% -> 0%
where the time goes in v1:
time: 88.6 us; the launch traced here: 88.4 us
  Pallas kernels  76.2 us (86%)
  local copies, waits for them, and re-layouts  7.69 us (9%)
  other arithmetic  3.87 us (4%)
    pallas_call x1, Pallas kernels, local(): pl.pallas_call(kernel, out_shape=(jax.ShapeDtypeStruct((2, 4, 96, 256), B...  76.2 us
    unnamed x18, local copies, waits for them, and re-layouts  4.68 us
    mul x1, other arithmetic, local(): dout[:27 * 192].reshape(27, 192, 128)[:, :, :96].astype(F32) * scale  1.8 us

profile of v1, /device:TPU:1, one launch (start us, length us, event | category | flops | bytes accessed | tf_op | source)
XLA Modules:
  0.0 88.4 jit_solution(10610222524987946092)
XLA Ops:
  0.6 0.0 copy-start
  0.6 2.6 %copy.11 = bf16[27,192,96]{1,2,0:T(8,128)(2,1)} copy(bf16[27,192,96]{2,1,0:T(8,128)(2,1)} %wd.1) | data formatting | bytes 1990656 | tf_op args[3]
  3.3 0.0 copy-done
  3.3 0.0 copy-start.6
  3.3 0.0 copy-start.2
  3.3 0.3 copy.10
  3.6 0.0 copy-start.4
  3.6 0.9 reverse_bitcast_fusion.wft
  4.5 0.0 copy-done.6
  4.5 0.0 copy-done.2
  4.5 0.8 fusion.1.xm
  5.3 0.0 copy-done.4
  5.3 0.7 copy.17
  6.0 76.2 %section.1 = (bf16[2,4,96,256]{3,2,1,0:T(8,128)(2,1)}, bf16[192,256]{1,0:T(8,128)(2,1)}, bf16[5632,128]{1,0:T(8,128)(2,1)}, bf16[3072,128]{1,0:T(8,128)(2,1)}) custom-call(bf16[2,4,96,256]{3,2,1,0:T(8,128)(2,1)} %fusion.1.xm, s32[2,4,256]{2,1,0:T(4,128)} %bitcast.29, bf16[27,96,96]{2,1,0:T(8,128)(2,1)} %wf.1, bf16[27,96,96]{2,1,0:T(8,128)(2,1)} %reverse_bitcast_fusion.wft, ...), custom_call_target="tpu_custom_call" | custom-call | tf_op jit(solution)/shard_map/section/pallas_call | solution.py:428
  82.2 1.4 %slice.14 = bf16[5184,128]{1,0:T(8,128)(2,1)S(1)} slice(bf16[5632,128]{1,0:T(8,128)(2,1)} %get-tuple-element.11), slice={[0:5184], [0:128]} | slice | bytes 2654208 | tf_op jit(solution)/shard_map/slice | solution.py:461
  83.6 0.0 copy-start.1
  83.6 1.8 %convert_multiply_fusion = f32[27,192,96]{2,1,0:T(8,128)} fusion(bf16[27,192,128]{2,1,0:T(8,128)(2,1)S(1)} %bitcast.23), kind=kLoop, calls=%fused_computation | loop fusion | flops 995328 | bytes 2985984 | tf_op jit(solution)/shard_map/mul | solution.py:461
  85.4 0.0 copy-done.1
  85.5 0.0 copy-start.3
  85.5 0.0 copy-start.5
  85.5 1.2 %convert_multiply_fusion.1 = f32[27,96,96]{2,1,0:T(8,128)} fusion(bf16[27,96,128]{2,1,0:T(8,128)(2,1)S(1)} %bitcast.24), kind=kLoop, calls=%fused_computation.1 | loop fusion | flops 497664 | bytes 1492992 | tf_op jit(solution)/shard_map/mul | solution.py:462
  86.7 0.0 copy-done.3
  86.7 1.1 %copy.13 = bf16[1,96,2,4,256]{4,3,2,1,0:T(4,128)(2,1)} copy(bf16[1,96,2,4,256]{4,1,3,2,0:T(8,128)(2,1)S(1)} %bitcast.25) | data formatting | bytes 786432
  87.8 0.0 copy-done.5
  87.8 0.7 reshape.19
  (2 shorter events, 0.0 us)
Async XLA Ops:
  0.6 2.6 %copy-start = (bf16[27,96,96]{2,1,0:T(8,128)(2,1)S(1)}, bf16[27,96,96]{2,1,0:T(8,128)(2,1)}, u32[]{:S(2)}) copy-start(bf16[27,96,96]{2,1,0:T(8,128)(2,1)} %wf.1) | copy-start | bytes 1492996
  3.3 1.2 %copy-start.6 = (s32[1,2,4,256]{3,2,1,0:T(4,128)S(1)}, s32[1,2,4,256]{3,2,1,0:T(4,128)}, u32[]{:S(2)}) copy-start(s32[1,2,4,256]{3,2,1,0:T(4,128)} %param.6) | copy-start | bytes 24580
  3.3 1.2 %copy-start.2 = (bf16[1,96,2,4,256]{4,3,2,1,0:T(4,128)(2,1)S(1)}, bf16[1,96,2,4,256]{4,3,2,1,0:T(4,128)(2,1)}, u32[]{:S(2)}) copy-start(bf16[1,96,2,4,256]{4,3,2,1,0:T(4,128)(2,1)} %param.5) | copy-start | bytes 1179652
  3.6 1.8 %copy-start.4 = (bf16[1,192,1,2,128]{4,3,2,1,0:T(2,128)(2,1)S(1)}, bf16[1,192,1,2,128]{4,3,2,1,0:T(2,128)(2,1)}, u32[]{:S(2)}) copy-start(bf16[1,192,1,2,128]{4,3,2,1,0:T(2,128)(2,1)} %param.9) | copy-start | bytes 294916
  83.6 1.8 %copy-start.1 = (bf16[3072,128]{1,0:T(8,128)(2,1)S(1)}, bf16[3072,128]{1,0:T(8,128)(2,1)}, u32[]{:S(2)}) copy-start(bf16[3072,128]{1,0:T(8,128)(2,1)} %get-tuple-element.10) | copy-start | bytes 2359300
  85.5 1.2 %copy-start.3 = (bf16[2,4,96,256]{3,2,1,0:T(8,128)(2,1)S(1)}, bf16[2,4,96,256]{3,2,1,0:T(8,128)(2,1)}, u32[]{:S(2)}) copy-start(bf16[2,4,96,256]{3,2,1,0:T(8,128)(2,1)} %get-tuple-element.9) | copy-start | bytes 1179652
  85.5 2.3 %copy-start.5 = (bf16[192,256]{1,0:T(8,128)(2,1)S(1)}, bf16[192,256]{1,0:T(8,128)(2,1)}, u32[]{:S(2)}) copy-start(bf16[192,256]{1,0:T(8,128)(2,1)} %get-tuple-element.8) | copy-start | bytes 294916

commit v2 on v1

v2 whole, which is shorter than its diff:
```python
import jax
import jax.numpy as jnp
from jax import lax
from jax.experimental import pallas as pl
from jax.experimental.pallas import tpu as pltpu
from jax.sharding import PartitionSpec as P

BF = jnp.bfloat16
F32 = jnp.float32
NT = (((1,), (1,)), ((), ()))
HD = 128
HF = 64


def mm(a, b):
    return jnp.dot(a, b, preferred_element_type=F32)


def mm_nt(a, b):
    return lax.dot_general(a, b, NT, preferred_element_type=F32)


def lane_ids(shape):
    return lax.broadcasted_iota(jnp.int32, shape, 1)


def from_before(v):
    return jnp.where(lane_ids(v.shape) == 0, 0.0, pltpu.roll(v, 1, 1))


def from_after(v):
    n = v.shape[1]
    return jnp.where(lane_ids(v.shape) == n - 1, 0.0, pltpu.roll(v, n - 1, 1))


def split_z(n):
    r = lax.broadcasted_iota(jnp.int32, (n, n), 0)
    c = lax.broadcasted_iota(jnp.int32, (n, n), 1)
    src = jnp.where(c < n // 2, 2 * c, 2 * c - n + 1)
    return (r == src).astype(F32).astype(BF)


def join_z(n):
    r = lax.broadcasted_iota(jnp.int32, (n, n), 0)
    c = lax.broadcasted_iota(jnp.int32, (n, n), 1)
    src = jnp.where(r < n // 2, 2 * r, 2 * r - n + 1)
    return (c == src).astype(F32).astype(BF)


def gather_dz(acc, c):
    a0, a1, a2 = acc[:c], acc[c : 2 * c], acc[2 * c :]
    even = from_before(a0[:, 128:]) + a1[:, :128] + a2[:, 128:]
    odd = a0[:, :128] + a1[:, 128:] + from_after(a2[:, :128])
    return jnp.concatenate([even, odd], axis=1)


class Place:
    def __init__(self):
        self.slab = lax.axis_index("slab")
        self.rep = lax.axis_index("rep")
        self.core = self.slab % 2
        self.x = (self.slab // 2) % 4
        self.zlo = self.slab // 8
        self.y = self.rep % 4
        self.zhi = self.rep // 4
        self.z = self.zhi * 4 + self.zlo

    def at(self, core, x, y, z):
        return {"slab": (z % 4) * 8 + x * 2 + core, "rep": (z // 4) * 4 + y}

    def partner(self):
        return self.at(1 - self.core, self.x, self.y, self.z)

    def plane(self, k, sign=1):
        x = (self.x + sign * (k // 4) + 4) % 4
        y = (self.y + sign * (k % 4) + 4) % 4
        return x, y

    def plane_dev(self, k):
        x, y = self.plane(k)
        return self.at(self.core, x, y, self.z)

    def z_dev(self, k):
        return self.at(self.core, self.x, self.y, (self.z + k) % 8)


def remote(src, dst, ssem, rsem, dev):
    return pltpu.make_async_remote_copy(
        src_ref=src, dst_ref=dst, send_sem=ssem, recv_sem=rsem, device_id=dev,
        device_id_type=pl.DeviceIdType.MESH,
    )


class Sum:
    def __init__(self, at, h, part, out, cbuf, acc, rs, zb, sems):
        self.at, self.h = at, h
        self.part, self.out, self.cbuf, self.acc, self.rs, self.zb = part, out, cbuf, acc, rs, zb
        self.ss, self.rr = sems
        self.sent = []

    def rows(self, start):
        return pl.ds(pl.multiple_of(start, 16), self.h)

    def copy(self, src, dst, i, dev):
        c = remote(src, dst, self.ss.at[i], self.rr.at[i], dev)
        c.start()
        self.sent.append(c)
        return c

    def half(self, core):
        return pl.ds(pl.multiple_of(core * (16 * self.h), 16), 16 * self.h)

    def one(self):
        self.c1 = self.copy(self.part.at[self.half(1 - self.at.core)], self.cbuf, 0, self.at.partner())

    def two(self):
        self.c1.wait_recv()
        h, at = self.h, self.at
        self.c2 = []
        for k in list(range(1, 16)) + [0]:
            x, y = at.plane(k)
            m = x * 4 + y
            mine = self.part[self.rows(at.core * (16 * h) + m * h), :].astype(F32)
            both = mine + self.cbuf[self.rows(m * h), :].astype(F32)
            self.acc[self.rows(m * h), :] = both.astype(BF)
            if k:
                self.c2.append(self.copy(self.acc.at[self.rows(m * h)], self.rs.at[k], k, at.plane_dev(k)))

    def three(self):
        h, at = self.h, self.at
        total = self.acc[self.rows((at.x * 4 + at.y) * h), :].astype(F32)
        for k in range(1, 16):
            self.c2[k - 1].wait_recv()
            total = total + self.rs[k].astype(F32)
        self.zb[at.z] = total.astype(BF)
        self.c3 = [
            self.copy(self.zb.at[at.z], self.zb.at[at.z], 16 + k, at.z_dev(k)) for k in range(1, 8)
        ]

    def four(self):
        h, at = self.h, self.at
        for c in self.c3:
            c.wait_recv()
        total = self.zb[0].astype(F32)
        for k in range(1, 8):
            total = total + self.zb[k].astype(F32)
        mine = self.rows(at.core * (16 * h) + (at.x * 4 + at.y) * h)
        self.out[mine, :] = total.astype(BF)
        self.c4 = [
            self.copy(self.out.at[mine], self.out.at[mine], 24 + k, at.plane_dev(k)) for k in range(1, 16)
        ]
        self.c5 = [self.copy(self.out.at[mine], self.out.at[mine], 40, at.partner())]

    def five(self):
        h, at = self.h, self.at
        for k in range(1, 16):
            self.c4[k - 1].wait_recv()
            x, y = at.plane(k, -1)
            rows = self.rows(at.core * (16 * h) + (x * 4 + y) * h)
            self.c5.append(self.copy(self.out.at[rows], self.out.at[rows], 40 + k, at.partner()))

    def six(self):
        for c in self.c5:
            c.wait_recv()
        for c in self.sent:
            c.wait_send()


def packed(ref, rows, tile, slot):
    tile, off = tile + 96 * slot // 128, 96 * slot % 128
    a = ref[rows * tile : rows * tile + rows, :]
    if off == 0:
        return a[:, :96]
    if off == 32:
        return a[:, 32:]
    b = ref[rows * (tile + 1) : rows * (tile + 1) + rows, :]
    return jnp.concatenate([a[:, off:], b[:, : off - 32]], axis=1)


def put_tiles(ref, rows, tile, v):
    extra = -v.shape[1] % 128
    if extra:
        v = jnp.concatenate([v, jnp.zeros((rows, extra), v.dtype)], axis=1)
    for i in range(v.shape[1] // 128):
        ref[rows * (tile + i) : rows * (tile + i) + rows, :] = v[:, 128 * i : 128 * i + 128].astype(BF)


def kernel(
    xm, occ, wf, wd, cot,
    gf, so, dout, fout,
    xb, gb, hs, ds, part, kf, kb, kd, kt, gs, gp, gn, bp, bn, raw,
    dpart, dfull, dcb, dacc, drs, dzb, fpart, ffull, fcb, facc, frs, fzb,
    hs_s, hs_r, dsem_s, dsem_r, fsem_s, fsem_r,
):
    at = Place()
    first, last = at.slab == 0, at.slab == 31
    left = {"slab": jnp.maximum(at.slab - 1, 0), "rep": at.rep}
    right = {"slab": jnp.minimum(at.slab + 1, 31), "rep": at.rep}
    barrier = pltpu.get_barrier_semaphore()

    def greet(dev):
        pl.semaphore_signal(barrier, 1, device_id=dev, device_id_type=pl.DeviceIdType.MESH)

    @pl.when(jnp.logical_not(first))
    def _():
        greet(left)

    @pl.when(jnp.logical_not(last))
    def _():
        greet(right)

    for k in range(1, 16):
        greet(at.plane_dev(k))
    for k in range(1, 8):
        greet(at.z_dev(k))

    class Edge:
        def __init__(self, i, to_left=None, to_right=None):
            self.l = self.r = None
            if to_left is not None:
                self.l = remote(*to_left, hs_s.at[i], hs_r.at[i], left)
                self.lz = to_left[1]
            if to_right is not None:
                self.r = remote(*to_right, hs_s.at[i + 1], hs_r.at[i + 1], right)
                self.rz = to_right[1]

        def start(self):
            if self.l is not None:
                pl.when(jnp.logical_not(first))(self.l.start)
            if self.r is not None:
                pl.when(jnp.logical_not(last))(self.r.start)

        def from_right(self):
            pl.when(jnp.logical_not(last))(self.l.wait_recv)

            @pl.when(last)
            def _():
                self.lz[...] = jnp.zeros(self.lz.shape, BF)

        def from_left(self):
            pl.when(jnp.logical_not(first))(self.r.wait_recv)

            @pl.when(first)
            def _():
                self.rz[...] = jnp.zeros(self.rz.shape, BF)

        def done(self):
            if self.l is not None:
                pl.when(jnp.logical_not(first))(self.l.wait_send)
            if self.r is not None:
                pl.when(jnp.logical_not(last))(self.r.wait_send)

    inner = (pl.ds(1, 4), slice(None))
    edge_x = Edge(0, (xm.at[0], raw.at[1]), (xm.at[1], raw.at[0]))
    edge_b = Edge(2, to_right=(bp, bn))
    edge_g = Edge(4, to_left=(gp, gn))
    edge_d = Edge(6, (gb.at[(1,) + inner], gb.at[(3,) + inner]), (gb.at[(2,) + inner], gb.at[(0,) + inner]))

    pz = split_z(256)
    masks = [mm(occ[p].astype(F32).astype(BF), pz) for p in range(2)]
    mask = lambda p, q: masks[p][q : q + 1]
    for p in range(2):
        for q in range(4):
            xb[1 + p, 1 + q] = mm(xm[p, q], pz).astype(BF)
    for b in (xb, gb):
        for p in range(4):
            b[p, 0] = jnp.zeros((96, 256), BF)
            b[p, 5] = jnp.zeros((96, 256), BF)
    for dx in range(3):
        for dy in range(3):
            base = 384 * dx + 96 * dy
            kf[:, base : base + 96] = wf[9 * dx + 3 * dy : 9 * dx + 3 * dy + 3].reshape(288, 96)
        kf[:, 384 * dx + 288 : 384 * dx + 384] = jnp.zeros((288, 96), BF)

    pl.semaphore_wait(barrier, 22 + jnp.where(first, 0, 1) + jnp.where(last, 0, 1))
    edge_x.start()

    gap = jnp.zeros((96, 256), BF)

    def rows_of(b, p, q):
        return [b[p, q + dy] for dy in range(3)]

    for p in range(2):
        for q in range(4):
            stack = jnp.concatenate(rows_of(xb, 1, q) + [gap] + rows_of(xb, 2, q), axis=0)
            base = 384 * (1 - p)
            part[p, q] = mm(kf[:, base : base + 672], stack)

    eye = (lax.broadcasted_iota(jnp.int32, (96, 96), 0) == lax.broadcasted_iota(jnp.int32, (96, 96), 1))
    eye = eye.astype(F32).astype(BF)
    for o in range(27):
        kd[o // 9, :, 96 * (o % 9) : 96 * (o % 9) + 96] = wd[o]
        kt[o] = mm_nt(eye, wd[o]).astype(BF)
        kb[96 * (o % 3) : 96 * (o % 3) + 96, 96 * (o // 3) : 96 * (o // 3) + 96] = mm_nt(eye, wf[26 - o]).astype(BF)

    def finish(p):
        for q in range(4):
            xb[3 * p, 1 + q] = mm(raw[p, q], pz).astype(BF)
        for q in range(4):
            base = 768 * p
            halo = mm(kf[:, base : base + 288], jnp.concatenate(rows_of(xb, 3 * p, q), axis=0))
            pre = gather_dz(part[p, q] + halo, 96)
            sig = jax.nn.sigmoid(pre)
            h = (pre * sig * mask(p, q)).astype(BF).astype(F32)
            ds[p, q] = mask(p, q) * (sig * (1.0 + pre * (1.0 - sig)))
            even, odd = h[:, :128].astype(BF), h[:, 128:].astype(BF)
            before = from_before(h[:, 128:]).astype(BF)
            for dy in range(3):
                if (q + 1 - dy) % 2 == 0 and 0 <= (q + 1 - dy) // 2 < 2:
                    j = (q + 1 - dy) // 2
                    lanes = slice(128 * j, 128 * j + 128)
                    for dz, v in enumerate((before, even, odd)):
                        row = 96 * (9 * p + 3 * dy + dz)
                        hs[row : row + 96, lanes] = v

    hs_zero = jnp.zeros((288, 128), BF)
    for p in range(2):
        hs[864 * p : 864 * p + 288, :128] = hs_zero
    edge_x.from_right()
    finish(1)
    bp[...] = mm(kd[0], hs[864:1728, :]).astype(BF)
    edge_b.start()
    edge_x.from_left()
    finish(0)
    down = mm(kd[1], hs[:864, :]) + mm(kd[2], hs[864:1728, :])
    order = join_z(384)
    cots = mm(order, cot[...])
    cots = jnp.concatenate([cots[:192], cots[192:]], axis=1)
    coarse = []
    for j in range(2):
        m = [mask(p, 2 * j + q) for p in range(2) for q in range(2)]
        m = jnp.maximum(jnp.maximum(m[0], m[1]), jnp.maximum(m[2], m[3]))
        coarse.append(jnp.maximum(m[:, :128], m[:, 128:]))
    cm = jnp.concatenate(coarse, axis=1)
    edge_b.from_left()
    down = down + bn[...].astype(F32)
    sig = jax.nn.sigmoid(down)
    gp[...] = (cots * cm * (sig * (1.0 + down * (1.0 - sig)))).astype(BF)
    edge_g.start()
    out = (down * sig * cm).astype(BF)
    out = jnp.concatenate([out[:, :128], out[:, 128:]], axis=0)
    so[...] = mm(split_z(384), out).astype(BF)

    dsum = Sum(at, HD, dpart, dfull, dcb, dacc, drs, dzb, (dsem_s, dsem_r))
    fsum = Sum(at, HF, fpart, ffull, fcb, facc, frs, fzb, (fsem_s, fsem_r))
    for n in range(0, 1728, 768):
        put_tiles(dpart, 192, n // 128, mm_nt(gp[...], hs[n : min(n + 768, 1728), :]))
    dpart[21 * 192 :, :] = jnp.zeros((32 * HD - 21 * 192, 128), BF)

    def back(dx, g):
        r = mm(kt[9 * dx : 9 * dx + 9].reshape(864, 192), g[...])
        out = []
        for q, terms in enumerate((((0, 1),), ((0, 2), (1, 0)), ((1, 1),), ((1, 2),))):
            even, odd = 0.0, 0.0
            for j, dy in terms:
                lanes = slice(128 * j, 128 * j + 128)
                r0, r1, r2 = [r[96 * (3 * dy + dz) : 96 * (3 * dy + dz) + 96, lanes] for dz in range(3)]
                even = even + r1
                odd = odd + r2 + from_after(r0)
            out.append(jnp.concatenate([even, odd], axis=1))
        return out

    for q, v in enumerate(back(1, gp)):
        gb[1, 1 + q] = (v * ds[0, q]).astype(BF)
    own = back(2, gp)
    edge_g.from_right()
    for n in range(0, 864, 768):
        put_tiles(dpart, 192, 14 + n // 128, mm_nt(gn[...], hs[864 + n : 864 + min(n + 768, 864), :]))
    dsum.one()
    nxt = back(0, gn)
    for q in range(4):
        gb[2, 1 + q] = ((own[q] + nxt[q]) * ds[1, q]).astype(BF)
    edge_d.start()

    for p in range(2):
        for q in range(4):
            g = gb[1 + p, 1 + q].astype(F32)
            ge, go = g[:, :128], g[:, 128:]
            base = 256 * (4 * p + q)
            gs[0:96, base : base + 128] = go.astype(BF)
            gs[0:96, base + 128 : base + 256] = from_after(ge).astype(BF)
            gs[96:192, base : base + 256] = g.astype(BF)
            gs[192:288, base : base + 128] = from_before(go).astype(BF)
            gs[192:288, base + 128 : base + 256] = ge.astype(BF)
    dsum.two()
    for j0 in range(0, 9, 4):
        rhs = jnp.concatenate(
            [
                jnp.concatenate([xb[p + j // 3, q + j % 3] for p in range(2) for q in range(4)], axis=1)
                for j in range(j0, min(j0 + 4, 9))
            ],
            axis=0,
        )
        put_tiles(fpart, 288, 3 * (j0 // 4), mm_nt(gs[...], rhs))
    fpart[7 * 288 :, :] = jnp.zeros((32 * HF - 7 * 288, 128), BF)
    fsum.one()
    edge_d.from_right()
    edge_d.from_left()

    jz = join_z(256)

    def grad_plane(p):
        for q in range(4):
            stack = jnp.concatenate([r for dx in range(3) for r in rows_of(gb, p + dx, q)], axis=0)
            g = (gather_dz(mm(kb[...], stack), 96) * mask(p, q)).astype(BF)
            gf[p, q] = mm(g, jz).astype(BF)

    grad_plane(0)
    fsum.two()
    grad_plane(1)
    dsum.three()
    fsum.three()
    dsum.four()
    fsum.four()
    dsum.five()
    fsum.five()
    dsum.six()
    for o in range(27):
        dout[o] = packed(dfull, 192, 14 if o < 9 else 0, o if o < 9 else o - 9)
    fsum.six()
    for j in range(9):
        fout[3 * j : 3 * j + 3] = packed(ffull, 288, 0, j).reshape(3, 96, 96)
    for e in (edge_x, edge_b, edge_g, edge_d):
        e.done()


def local(features, occupancy, w_fine, w_down, cotangent):
    mask = occupancy[0].astype(F32)
    masked = (features[0] * mask).astype(BF)
    xm = jnp.transpose(masked, (1, 2, 0, 3))
    cot = cotangent.reshape(384, 128)
    vm = pl.BlockSpec(memory_space=pltpu.VMEM)

    def sums(h):
        return [
            pltpu.VMEM((32 * h, 128), BF), pltpu.VMEM((32 * h, 128), BF), pltpu.VMEM((16 * h, 128), BF),
            pltpu.VMEM((16 * h, 128), BF), pltpu.VMEM((16, h, 128), BF), pltpu.VMEM((8, h, 128), BF),
        ]

    dma = pltpu.SemaphoreType.DMA
    gf, so, dout, fout = pl.pallas_call(
        kernel,
        out_shape=(
            jax.ShapeDtypeStruct((2, 4, 96, 256), BF),
            jax.ShapeDtypeStruct((384, 128), BF),
            jax.ShapeDtypeStruct((27, 192, 96), BF),
            jax.ShapeDtypeStruct((27, 96, 96), BF),
        ),
        in_specs=[vm] * 5,
        out_specs=(vm,) * 4,
        scratch_shapes=[
            pltpu.VMEM((4, 6, 96, 256), BF),
            pltpu.VMEM((4, 6, 96, 256), BF),
            pltpu.VMEM((18 * 96, 256), BF),
            pltpu.VMEM((2, 4, 96, 256), F32),
            pltpu.VMEM((2, 4, 288, 256), F32),
            pltpu.VMEM((288, 1152), BF),
            pltpu.VMEM((288, 864), BF),
            pltpu.VMEM((3, 192, 864), BF),
            pltpu.VMEM((27, 96, 192), BF),
            pltpu.VMEM((288, 2048), BF),
            pltpu.VMEM((192, 256), BF),
            pltpu.VMEM((192, 256), BF),
            pltpu.VMEM((192, 256), BF),
            pltpu.VMEM((192, 256), BF),
            pltpu.VMEM((2, 4, 96, 256), BF),
        ]
        + sums(HD)
        + sums(HF)
        + [dma((8,)), dma((8,)), dma((56,)), dma((56,)), dma((56,)), dma((56,))],
        compiler_params=pltpu.CompilerParams(
            collective_id=0, has_side_effects=True, vmem_limit_bytes=60 * 2**20
        ),
        name="section",
    )(xm, occupancy[0], w_fine, w_down, cot)
    scale = 1.0 / jnp.sqrt(jnp.float32(65536))
    return (
        so.reshape(1, 192, 1, 2, 128),
        jnp.transpose(gf, (2, 0, 1, 3))[None],
        fout.astype(F32) * scale,
        dout.astype(F32) * scale,
    )


def solution(mesh):
    return jax.shard_map(
        local,
        mesh=mesh,
        in_specs=(
            P("rep", None, "slab", None, None),
            P("rep", "slab", None, None),
            P(),
            P(),
            P("rep", None, "slab", None, None),
        ),
        out_specs=(
            P("rep", None, "slab", None, None),
            P("rep", None, "slab", None, None),
            P(),
            P(),
        ),
        check_vma=False,
    )
```

time: 88.6 us -> 73.6 us (0.83)
  Pallas kernels: 76.2 us -> 64.1 us
  local copies, waits for them, and re-layouts: 7.69 us -> 1.7 us
  other arithmetic: 3.87 us -> 6.94 us
    pallas_call x1, Pallas kernels: 76.2 us -> 64.1 us  [local(): pl.pallas_call(kernel, out_shape=(jax.ShapeDtypeStruct((2, 4, 96, 256), B...]
    unnamed x18 -> x8, local copies, waits for them, and re-layouts: 4.68 us -> 1.7 us
    slice x2 -> x0, local copies, waits for them, and re-layouts: 1.45 us -> none  [the longest x1 1.41 us: local(): dout[:27 * 192].reshape(27, 192, 128)[:, :, :96].astype(F32) * scale]
    mul x2, other arithmetic: 3.02 us -> 4.41 us  [the longest x1 3.19 us: local(): dout.astype(F32) * scale]
    transpose x1, other arithmetic: 0.84 us -> 1.83 us  [local(): xm = jnp.transpose(masked, (1, 2, 0, 3))]
where the time goes in v2:
time: 73.6 us; the launch traced here: 73.4 us
  Pallas kernels  64.1 us (87%)
  other arithmetic  6.94 us (9%)
  local copies, waits for them, and re-layouts  1.7 us (2%)
    pallas_call x1, Pallas kernels, local(): pl.pallas_call(kernel, out_shape=(jax.ShapeDtypeStruct((2, 4, 96, 256), B...  64.1 us
    mul x1, other arithmetic, local(): dout.astype(F32) * scale  3.19 us
    transpose x1, other arithmetic, local(): xm = jnp.transpose(masked, (1, 2, 0, 3))  1.83 us
    unnamed x8, local copies, waits for them, and re-layouts  1.7 us

profile of v2, /device:TPU:1, one launch (start us, length us, event | category | flops | bytes accessed | tf_op | source)
XLA Modules:
  0.0 73.4 jit_solution(16336697371004024955)
XLA Ops:
  0.6 0.7 convert_bitcast_fusion
  1.3 1.8 %fusion.1.xm = bf16[2,4,96,256]{3,2,1,0:T(8,128)(2,1)} fusion(bf16[1,96,2,4,256]{4,3,2,1,0:T(4,128)(2,1)} %param.5, f32[2,4,256]{2,1,0:T(4,128)S(1)} %convert_bitcast_fusion), kind=kLoop, calls=%fused_computation.4 | loop fusion | flops 589824 | bytes 794624 | tf_op jit(solution)/shard_map/transpose | solution.py:430
  3.2 64.1 %section.1 = (bf16[2,4,96,256]{3,2,1,0:T(8,128)(2,1)}, bf16[384,128]{1,0:T(8,128)(2,1)}, bf16[27,192,96]{2,1,0:T(8,128)(2,1)}, bf16[27,96,96]{2,1,0:T(8,128)(2,1)}) custom-call(bf16[2,4,96,256]{3,2,1,0:T(8,128)(2,1)} %fusion.1.xm, s32[2,4,256]{2,1,0:T(4,128)} %bitcast.18, bf16[27,96,96]{2,1,0:T(8,128)(2,1)} %wf.1, bf16[27,192,96]{2,1,0:T(8,128)(2,1)} %wd.1, ...), custom_call_target="tpu_custom_call" | custom-call | tf_op jit(solution)/shard_map/section/pallas_call | solution.py:441
  67.3 0.0 copy-start
  67.3 3.2 %convert_multiply_fusion = f32[27,192,96]{2,1,0:T(8,128)} fusion(bf16[27,192,96]{2,1,0:T(8,128)(2,1)} %get-tuple-element.11), kind=kLoop, calls=%fused_computation | loop fusion | flops 995328 | bytes 2985984 | tf_op jit(solution)/shard_map/mul | solution.py:481
  70.5 0.0 copy-start.1
  70.5 0.0 copy-done
  70.5 0.0 copy-start.2
  70.5 1.2 %convert_multiply_fusion.1 = f32[27,96,96]{2,1,0:T(8,128)} fusion(bf16[27,96,96]{2,1,0:T(8,128)(2,1)S(1)} %copy-done), kind=kLoop, calls=%fused_computation.1 | loop fusion | flops 497664 | bytes 1492992 | tf_op jit(solution)/shard_map/mul | solution.py:480
  71.7 0.0 copy-done.1
  71.7 1.1 %copy.11 = bf16[1,96,2,4,256]{4,3,2,1,0:T(4,128)(2,1)} copy(bf16[1,96,2,4,256]{4,1,3,2,0:T(8,128)(2,1)S(1)} %bitcast.15) | data formatting | bytes 786432
  72.8 0.0 copy-done.2
  72.8 0.6 copy.14
Async XLA Ops:
  67.3 3.2 %copy-start = (bf16[27,96,96]{2,1,0:T(8,128)(2,1)S(1)}, bf16[27,96,96]{2,1,0:T(8,128)(2,1)}, u32[]{:S(2)}) copy-start(bf16[27,96,96]{2,1,0:T(8,128)(2,1)} %get-tuple-element.10) | copy-start | bytes 1492996
  70.5 1.2 %copy-start.1 = (bf16[2,4,96,256]{3,2,1,0:T(8,128)(2,1)S(1)}, bf16[2,4,96,256]{3,2,1,0:T(8,128)(2,1)}, u32[]{:S(2)}) copy-start(bf16[2,4,96,256]{3,2,1,0:T(8,128)(2,1)} %get-tuple-element.9) | copy-start | bytes 1179652
  70.5 2.3 %copy-start.2 = (bf16[384,128]{1,0:T(8,128)(2,1)S(1)}, bf16[384,128]{1,0:T(8,128)(2,1)}, u32[]{:S(2)}) copy-start(bf16[384,128]{1,0:T(8,128)(2,1)} %get-tuple-element.8) | copy-start | bytes 294916

commit v3 on v2

--- a/solution.py
+++ b/solution.py
@@ -92,75 +92,135 @@
 
 
 class Sum:
-    def __init__(self, at, h, part, out, cbuf, acc, rs, zb, sems):
-        self.at, self.h = at, h
-        self.part, self.out, self.cbuf, self.acc, self.rs, self.zb = part, out, cbuf, acc, rs, zb
+    def __init__(self, at, h, cut_z, part, out, cbuf, acc, r1, s2, r2, zb, zr, sems):
+        self.at, self.h, self.cut_z = at, h, cut_z
+        self.part, self.out, self.cbuf, self.acc = part, out, cbuf, acc
+        self.r1, self.s2, self.r2, self.zb, self.zr = r1, s2, r2, zb, zr
         self.ss, self.rr = sems
         self.sent = []
-
-    def rows(self, start):
-        return pl.ds(pl.multiple_of(start, 16), self.h)
-
-    def copy(self, src, dst, i, dev):
+        self.base = at.core * (16 * h)
+        self.pos = (at.x, at.y)
+
+    def rows(self, start, n):
+        return pl.ds(pl.multiple_of(start, 8), n)
+
+    def copy(self, src, dst, dev):
+        i = len(self.sent)
         c = remote(src, dst, self.ss.at[i], self.rr.at[i], dev)
         c.start()
         self.sent.append(c)
         return c
 
-    def half(self, core):
-        return pl.ds(pl.multiple_of(core * (16 * self.h), 16), 16 * self.h)
+    def along(self, axis, d):
+        at = self.at
+        x, y = ((at.x + d) % 4, at.y) if axis == 0 else (at.x, (at.y + d) % 4)
+        return at.at(at.core, x, y, at.z)
 
     def one(self):
-        self.c1 = self.copy(self.part.at[self.half(1 - self.at.core)], self.cbuf, 0, self.at.partner())
+        src = self.part.at[self.rows((1 - self.at.core) * (16 * self.h), 16 * self.h)]
+        self.c1 = self.copy(src, self.cbuf, self.at.partner())
 
     def two(self):
         self.c1.wait_recv()
-        h, at = self.h, self.at
-        self.c2 = []
-        for k in list(range(1, 16)) + [0]:
-            x, y = at.plane(k)
-            m = x * 4 + y
-            mine = self.part[self.rows(at.core * (16 * h) + m * h), :].astype(F32)
-            both = mine + self.cbuf[self.rows(m * h), :].astype(F32)
-            self.acc[self.rows(m * h), :] = both.astype(BF)
-            if k:
-                self.c2.append(self.copy(self.acc.at[self.rows(m * h)], self.rs.at[k], k, at.plane_dev(k)))
+        h = self.h
+        self.c2 = [[], []]
+        for d in (2, 1, 3, 0):
+            for axis in range(2):
+                start = 8 * h * axis + ((self.pos[axis] + d) % 4) * (2 * h)
+                rows = self.rows(start, 2 * h)
+                both = self.part[self.rows(self.base + start, 2 * h), :].astype(F32) + self.cbuf[rows, :].astype(F32)
+                self.acc[rows, :] = both.astype(BF)
+                if d:
+                    self.c2[axis].append(self.copy(self.acc.at[rows], self.r1.at[axis, d], self.along(axis, d)))
 
     def three(self):
-        h, at = self.h, self.at
-        total = self.acc[self.rows((at.x * 4 + at.y) * h), :].astype(F32)
-        for k in range(1, 16):
-            self.c2[k - 1].wait_recv()
-            total = total + self.rs[k].astype(F32)
-        self.zb[at.z] = total.astype(BF)
-        self.c3 = [
-            self.copy(self.zb.at[at.z], self.zb.at[at.z], 16 + k, at.z_dev(k)) for k in range(1, 8)
-        ]
+        h = self.h
+        self.c3 = [[], []]
+        for axis in range(2):
+            for c in self.c2[axis]:
+                c.wait_recv()
+            total = self.acc[self.rows(8 * h * axis + self.pos[axis] * (2 * h), 2 * h), :].astype(F32)
+            for d in range(1, 4):
+                total = total + self.r1[axis, d].astype(F32)
+            self.s2[axis] = total.astype(BF)
+            for d in (2, 1, 3):
+                rows = self.rows(((self.pos[1 - axis] + d) % 4) * (h // 2), h // 2)
+                self.c3[axis].append(
+                    self.copy(self.s2.at[axis, rows], self.r2.at[axis, d], self.along(1 - axis, d))
+                )
 
     def four(self):
         h, at = self.h, self.at
-        for c in self.c3:
+        for axis in range(2):
+            for c in self.c3[axis]:
+                c.wait_recv()
+            total = self.s2[axis, self.rows(self.pos[1 - axis] * (h // 2), h // 2), :].astype(F32)
+            for d in range(1, 4):
+                total = total + self.r2[axis, d].astype(F32)
+            if self.cut_z:
+                self.zr[0, h // 2 * axis : h // 2 * axis + h // 2, :] = total.astype(BF)
+            else:
+                self.zb[at.z, h // 2 * axis : h // 2 * axis + h // 2, :] = total.astype(BF)
+        self.c4 = []
+        for k in (4, 3, 5, 2, 6, 1, 7):
+            if self.cut_z:
+                rows = self.rows(((at.z + k) % 8) * (h // 8), h // 8)
+                self.c4.append(self.copy(self.zr.at[0, rows], self.zr.at[k, pl.ds(0, h // 8)], at.z_dev(k)))
+            else:
+                self.c4.append(self.copy(self.zb.at[at.z], self.zb.at[at.z], at.z_dev(k)))
+
+    def five(self):
+        h, at = self.h, self.at
+        for c in self.c4:
+            c.wait_recv()
+        mine = self.rows(at.z * (h // 8), h // 8)
+        total = self.zr[0, mine, :].astype(F32)
+        for k in range(1, 8):
+            total = total + self.zr[k, : h // 8, :].astype(F32)
+        self.zb[0, mine, :] = total.astype(BF)
+        self.c4 = [
+            self.copy(self.zb.at[0, mine], self.zb.at[0, mine], at.z_dev(k)) for k in (4, 3, 5, 2, 6, 1, 7)
+        ]
+
+    def block(self, axis, pos):
+        return self.rows(self.base + 8 * self.h * axis + pos * (2 * self.h), 2 * self.h)
+
+    def six(self):
+        h = self.h
+        for c in self.c4:
             c.wait_recv()
         total = self.zb[0].astype(F32)
-        for k in range(1, 8):
-            total = total + self.zb[k].astype(F32)
-        mine = self.rows(at.core * (16 * h) + (at.x * 4 + at.y) * h)
-        self.out[mine, :] = total.astype(BF)
-        self.c4 = [
-            self.copy(self.out.at[mine], self.out.at[mine], 24 + k, at.plane_dev(k)) for k in range(1, 16)
-        ]
-        self.c5 = [self.copy(self.out.at[mine], self.out.at[mine], 40, at.partner())]
-
-    def five(self):
-        h, at = self.h, self.at
-        for k in range(1, 16):
-            self.c4[k - 1].wait_recv()
-            x, y = at.plane(k, -1)
-            rows = self.rows(at.core * (16 * h) + (x * 4 + y) * h)
-            self.c5.append(self.copy(self.out.at[rows], self.out.at[rows], 40 + k, at.partner()))
-
-    def six(self):
-        for c in self.c5:
+        if not self.cut_z:
+            for k in range(1, 8):
+                total = total + self.zb[k].astype(F32)
+        self.c6 = [[], []]
+        for axis in range(2):
+            start = self.base + 8 * h * axis + (self.pos[axis] * 4 + self.pos[1 - axis]) * (h // 2)
+            rows = self.rows(start, h // 2)
+            self.out[rows, :] = total[h // 2 * axis : h // 2 * axis + h // 2].astype(BF)
+            for d in (2, 1, 3):
+                self.c6[axis].append(self.copy(self.out.at[rows], self.out.at[rows], self.along(1 - axis, d)))
+
+    def seven(self):
+        self.c7, self.c8 = [[], []], []
+        for axis in range(2):
+            for c in self.c6[axis]:
+                c.wait_recv()
+            ref = self.out.at[self.block(axis, self.pos[axis])]
+            for d in (2, 1, 3):
+                self.c7[axis].append((d, self.copy(ref, ref, self.along(axis, d))))
+            self.c8.append(self.copy(ref, ref, self.at.partner()))
+
+    def eight(self):
+        for i in (1, 2, 0):
+            for axis in range(2):
+                d, c = self.c7[axis][i]
+                c.wait_recv()
+                ref = self.out.at[self.block(axis, (self.pos[axis] - d + 4) % 4)]
+                self.c8.append(self.copy(ref, ref, self.at.partner()))
+
+    def nine(self):
+        for c in self.c8:
             c.wait_recv()
         for c in self.sent:
             c.wait_send()
@@ -186,10 +246,10 @@
 
 
 def kernel(
-    xm, occ, wf, wd, cot,
+    xf, occ_far, wf_far, wd_far, cot_far,
     gf, so, dout, fout,
-    xb, gb, hs, ds, part, kf, kb, kd, kt, gs, gp, gn, bp, bn, raw,
-    dpart, dfull, dcb, dacc, drs, dzb, fpart, ffull, fcb, facc, frs, fzb,
+    xb, gb, hs, ds, part, kf, kb, kd, kt, gs, gp, gn, bp, bn, raw, rocc, occ, cot, wf, wd, near,
+    dpart, dfull, dcb, dacc, dr1, ds2, dr2, dzb, dzr, fpart, ffull, fcb, facc, fr1, fs2, fr2, fzb, fzr,
     hs_s, hs_r, dsem_s, dsem_r, fsem_s, fsem_r,
 ):
     at = Place()
@@ -235,14 +295,14 @@
 
             @pl.when(last)
             def _():
-                self.lz[...] = jnp.zeros(self.lz.shape, BF)
+                self.lz[...] = jnp.zeros(self.lz.shape, self.lz.dtype)
 
         def from_left(self):
             pl.when(jnp.logical_not(first))(self.r.wait_recv)
 
             @pl.when(first)
             def _():
-                self.rz[...] = jnp.zeros(self.rz.shape, BF)
+                self.rz[...] = jnp.zeros(self.rz.shape, self.rz.dtype)
 
         def done(self):
             if self.l is not None:
@@ -251,30 +311,40 @@
                 pl.when(jnp.logical_not(last))(self.r.wait_send)
 
     inner = (pl.ds(1, 4), slice(None))
-    edge_x = Edge(0, (xm.at[0], raw.at[1]), (xm.at[1], raw.at[0]))
+    edge_x = Edge(0, (xf.at[0], raw.at[1]), (xf.at[1], raw.at[0]))
+    edge_o = Edge(8, (occ_far.at[0], rocc.at[1]), (occ_far.at[1], rocc.at[0]))
     edge_b = Edge(2, to_right=(bp, bn))
     edge_g = Edge(4, to_left=(gp, gn))
     edge_d = Edge(6, (gb.at[(1,) + inner], gb.at[(3,) + inner]), (gb.at[(2,) + inner], gb.at[(0,) + inner]))
 
+    pl.semaphore_wait(barrier, 22 + jnp.where(first, 0, 1) + jnp.where(last, 0, 1))
+    edge_o.start()
+    edge_x.start()
+    pairs = ((occ_far, occ), (wf_far, wf), (wd_far, wd), (cot_far, cot))
+    load_o, load_f, load_d, load_c = [
+        pltpu.make_async_copy(a, b, near.at[i]) for i, (a, b) in enumerate(pairs)
+    ]
+    for c in (load_o, load_f, load_d, load_c):
+        c.start()
+
     pz = split_z(256)
+    load_o.wait()
     masks = [mm(occ[p].astype(F32).astype(BF), pz) for p in range(2)]
     mask = lambda p, q: masks[p][q : q + 1]
     for p in range(2):
         for q in range(4):
-            xb[1 + p, 1 + q] = mm(xm[p, q], pz).astype(BF)
+            xb[1 + p, 1 + q] = (mm(xf[p, q], pz) * mask(p, q)).astype(BF)
     for b in (xb, gb):
         for p in range(4):
             b[p, 0] = jnp.zeros((96, 256), BF)
             b[p, 5] = jnp.zeros((96, 256), BF)
+    load_f.wait()
     for dx in range(3):
         for dy in range(3):
             base = 384 * dx + 96 * dy
             kf[:, base : base + 96] = wf[9 * dx + 3 * dy : 9 * dx + 3 * dy + 3].reshape(288, 96)
         kf[:, 384 * dx + 288 : 384 * dx + 384] = jnp.zeros((288, 96), BF)
 
-    pl.semaphore_wait(barrier, 22 + jnp.where(first, 0, 1) + jnp.where(last, 0, 1))
-    edge_x.start()
-
     gap = jnp.zeros((96, 256), BF)
 
     def rows_of(b, p, q):
@@ -288,14 +358,24 @@
 
     eye = (lax.broadcasted_iota(jnp.int32, (96, 96), 0) == lax.broadcasted_iota(jnp.int32, (96, 96), 1))
     eye = eye.astype(F32).astype(BF)
-    for o in range(27):
-        kd[o // 9, :, 96 * (o % 9) : 96 * (o % 9) + 96] = wd[o]
-        kt[o] = mm_nt(eye, wd[o]).astype(BF)
-        kb[96 * (o % 3) : 96 * (o % 3) + 96, 96 * (o // 3) : 96 * (o // 3) + 96] = mm_nt(eye, wf[26 - o]).astype(BF)
+
+    def stack_kd(dx):
+        for o in range(9 * dx, 9 * dx + 9):
+            kd[dx, :, 96 * (o % 9) : 96 * (o % 9) + 96] = wd[o]
+
+    def stack_kt(dx):
+        for o in range(9 * dx, 9 * dx + 9):
+            kt[o] = mm_nt(eye, wd[o]).astype(BF)
+
+    load_d.wait()
+    stack_kd(0)
+    stack_kd(1)
+    stack_kd(2)
 
     def finish(p):
+        m = mm(rocc[p].astype(F32).astype(BF), pz)
         for q in range(4):
-            xb[3 * p, 1 + q] = mm(raw[p, q], pz).astype(BF)
+            xb[3 * p, 1 + q] = (mm(raw[p, q], pz) * m[q : q + 1]).astype(BF)
         for q in range(4):
             base = 768 * p
             halo = mm(kf[:, base : base + 288], jnp.concatenate(rows_of(xb, 3 * p, q), axis=0))
@@ -316,14 +396,17 @@
     hs_zero = jnp.zeros((288, 128), BF)
     for p in range(2):
         hs[864 * p : 864 * p + 288, :128] = hs_zero
+    edge_o.from_right()
     edge_x.from_right()
     finish(1)
     bp[...] = mm(kd[0], hs[864:1728, :]).astype(BF)
     edge_b.start()
+    edge_o.from_left()
     edge_x.from_left()
     finish(0)
     down = mm(kd[1], hs[:864, :]) + mm(kd[2], hs[864:1728, :])
     order = join_z(384)
+    load_c.wait()
     cots = mm(order, cot[...])
     cots = jnp.concatenate([cots[:192], cots[192:]], axis=1)
     coarse = []
@@ -332,17 +415,20 @@
         m = jnp.maximum(jnp.maximum(m[0], m[1]), jnp.maximum(m[2], m[3]))
         coarse.append(jnp.maximum(m[:, :128], m[:, 128:]))
     cm = jnp.concatenate(coarse, axis=1)
+    stack_kt(1)
     edge_b.from_left()
     down = down + bn[...].astype(F32)
     sig = jax.nn.sigmoid(down)
     gp[...] = (cots * cm * (sig * (1.0 + down * (1.0 - sig)))).astype(BF)
     edge_g.start()
+    stack_kt(2)
+    stack_kt(0)
     out = (down * sig * cm).astype(BF)
     out = jnp.concatenate([out[:, :128], out[:, 128:]], axis=0)
     so[...] = mm(split_z(384), out).astype(BF)
 
-    dsum = Sum(at, HD, dpart, dfull, dcb, dacc, drs, dzb, (dsem_s, dsem_r))
-    fsum = Sum(at, HF, fpart, ffull, fcb, facc, frs, fzb, (fsem_s, fsem_r))
+    dsum = Sum(at, HD, True, dpart, dfull, dcb, dacc, dr1, ds2, dr2, dzb, dzr, (dsem_s, dsem_r))
+    fsum = Sum(at, HF, False, fpart, ffull, fcb, facc, fr1, fs2, fr2, fzb, fzr, (fsem_s, fsem_r))
     for n in range(0, 1728, 768):
         put_tiles(dpart, 192, n // 128, mm_nt(gp[...], hs[n : min(n + 768, 1728), :]))
     dpart[21 * 192 :, :] = jnp.zeros((32 * HD - 21 * 192, 128), BF)
@@ -382,8 +468,9 @@
             gs[96:192, base : base + 256] = g.astype(BF)
             gs[192:288, base : base + 128] = from_before(go).astype(BF)
             gs[192:288, base + 128 : base + 256] = ge.astype(BF)
-    dsum.two()
     for j0 in range(0, 9, 4):
+        if j0 == 4:
+            dsum.two()
         rhs = jnp.concatenate(
             [
                 jnp.concatenate([xb[p + j // 3, q + j % 3] for p in range(2) for q in range(4)], axis=1)
@@ -394,6 +481,10 @@
         put_tiles(fpart, 288, 3 * (j0 // 4), mm_nt(gs[...], rhs))
     fpart[7 * 288 :, :] = jnp.zeros((32 * HF - 7 * 288, 128), BF)
     fsum.one()
+    for o in range(27):
+        kb[96 * (o % 3) : 96 * (o % 3) + 96, 96 * (o // 3) : 96 * (o // 3) + 96] = mm_nt(eye, wf[26 - o]).astype(BF)
+    fsum.two()
+    dsum.three()
     edge_d.from_right()
     edge_d.from_left()
 
@@ -406,35 +497,42 @@
             gf[p, q] = mm(g, jz).astype(BF)
 
     grad_plane(0)
-    fsum.two()
     grad_plane(1)
-    dsum.three()
+    dsum.four()
     fsum.three()
-    dsum.four()
     fsum.four()
     dsum.five()
-    fsum.five()
     dsum.six()
+    fsum.six()
+    dsum.seven()
+    fsum.seven()
+    dsum.eight()
+    fsum.eight()
+    dsum.nine()
     for o in range(27):
         dout[o] = packed(dfull, 192, 14 if o < 9 else 0, o if o < 9 else o - 9)
-    fsum.six()
+    fsum.nine()
     for j in range(9):
         fout[3 * j : 3 * j + 3] = packed(ffull, 288, 0, j).reshape(3, 96, 96)
-    for e in (edge_x, edge_b, edge_g, edge_d):
+    for e in (edge_x, edge_o, edge_b, edge_g, edge_d):
         e.done()
 
 
+def in_hbm(v):
+    return pltpu.with_memory_space_constraint(v, pltpu.HBM)
+
+
 def local(features, occupancy, w_fine, w_down, cotangent):
-    mask = occupancy[0].astype(F32)
-    masked = (features[0] * mask).astype(BF)
-    xm = jnp.transpose(masked, (1, 2, 0, 3))
+    xf = jnp.transpose(features[0], (1, 2, 0, 3))
     cot = cotangent.reshape(384, 128)
     vm = pl.BlockSpec(memory_space=pltpu.VMEM)
+    far = pl.BlockSpec(memory_space=pltpu.HBM)
 
     def sums(h):
         return [
             pltpu.VMEM((32 * h, 128), BF), pltpu.VMEM((32 * h, 128), BF), pltpu.VMEM((16 * h, 128), BF),
-            pltpu.VMEM((16 * h, 128), BF), pltpu.VMEM((16, h, 128), BF), pltpu.VMEM((8, h, 128), BF),
+            pltpu.VMEM((16 * h, 128), BF), pltpu.VMEM((2, 4, 2 * h, 128), BF), pltpu.VMEM((2, 2 * h, 128), BF),
+            pltpu.VMEM((2, 4, h // 2, 128), BF), pltpu.VMEM((8, h, 128), BF), pltpu.VMEM((8, h, 128), BF),
         ]
 
     dma = pltpu.SemaphoreType.DMA
@@ -446,7 +544,7 @@
             jax.ShapeDtypeStruct((27, 192, 96), BF),
             jax.ShapeDtypeStruct((27, 96, 96), BF),
         ),
-        in_specs=[vm] * 5,
+        in_specs=[vm, far, far, far, far],
         out_specs=(vm,) * 4,
         scratch_shapes=[
             pltpu.VMEM((4, 6, 96, 256), BF),
@@ -464,15 +562,21 @@
             pltpu.VMEM((192, 256), BF),
             pltpu.VMEM((192, 256), BF),
             pltpu.VMEM((2, 4, 96, 256), BF),
+            pltpu.VMEM((2, 4, 256), jnp.int32),
+            pltpu.VMEM((2, 4, 256), jnp.int32),
+            pltpu.VMEM((384, 128), BF),
+            pltpu.VMEM((27, 96, 96), BF),
+            pltpu.VMEM((27, 192, 96), BF),
+            dma((4,)),
         ]
         + sums(HD)
         + sums(HF)
-        + [dma((8,)), dma((8,)), dma((56,)), dma((56,)), dma((56,)), dma((56,))],
+        + [dma((10,)), dma((10,)), dma((56,)), dma((56,)), dma((56,)), dma((56,))],
         compiler_params=pltpu.CompilerParams(
-            collective_id=0, has_side_effects=True, vmem_limit_bytes=60 * 2**20
+            collective_id=0, has_side_effects=True, vmem_limit_bytes=32 * 2**20
         ),
         name="section",
-    )(xm, occupancy[0], w_fine, w_down, cot)
+    )(xf, in_hbm(occupancy[0]), in_hbm(w_fine), in_hbm(w_down), in_hbm(cot))
     scale = 1.0 / jnp.sqrt(jnp.float32(65536))
     return (
         so.reshape(1, 192, 1, 2, 128),

time: 73.6 us -> 67.5 us (0.917)
  other arithmetic: 6.94 us -> 3.02 us
  Pallas kernels: 64.1 us -> 60.9 us
  local copies, waits for them, and re-layouts: 1.7 us -> 2.76 us
    pallas_call x1, Pallas kernels: 64.1 us -> 60.9 us  [local(): pl.pallas_call(kernel, out_shape=(jax.ShapeDtypeStruct((2, 4, 96, 256), B...]
    transpose x1 -> x0, other arithmetic: 1.83 us -> none  [local(): xm = jnp.transpose(masked, (1, 2, 0, 3))]
    mul x1, other arithmetic: 3.19 us -> 1.81 us  [local(): dout.astype(F32) * scale]
    unnamed x8 -> x3, local copies, waits for them, and re-layouts: 1.7 us -> 2.76 us
where the time goes in v3:
time: 67.5 us; the launch traced here: 67.4 us
  Pallas kernels  60.9 us (90%)
  other arithmetic  3.02 us (4%)
  local copies, waits for them, and re-layouts  2.76 us (4%)
    pallas_call x1, Pallas kernels, local(): pl.pallas_call(kernel, out_shape=(jax.ShapeDtypeStruct((2, 4, 96, 256), B...  60.9 us
    unnamed x3, local copies, waits for them, and re-layouts  2.76 us
    mul x1, other arithmetic, local(): dout.astype(F32) * scale  1.81 us

profile of v3, /device:TPU:1, one launch (start us, length us, event | category | flops | bytes accessed | tf_op | source)
XLA Modules:
  0.0 67.4 jit_solution(13601124774048975430)
XLA Ops:
  0.6 1.1 %copy.13 = bf16[1,96,2,4,256]{4,1,3,2,0:T(8,128)(2,1)S(1)} copy(bf16[1,96,2,4,256]{4,3,2,1,0:T(4,128)(2,1)} %param.5) | data formatting | bytes 786432 | tf_op args[0]
  1.7 60.9 %section.1 = (bf16[2,4,96,256]{3,2,1,0:T(8,128)(2,1)S(1)}, bf16[384,128]{1,0:T(8,128)(2,1)S(1)}, bf16[27,192,96]{2,1,0:T(8,128)(2,1)S(1)}, bf16[27,96,96]{2,1,0:T(8,128)(2,1)S(1)}) custom-call(bf16[2,4,96,256]{3,2,1,0:T(8,128)(2,1)S(1)} %bitcast.13, s32[2,4,256]{2,1,0:T(4,128)} %bitcast.17, bf16[27,96,96]{2,1,0:T(8,128)(2,1)} %wf_far.1, ...), custom_call_target="tpu_custom_call" | custom-call | tf_op jit(solution)/shard_map/section/pallas_call | solution.py:539
  62.7 1.8 %convert_multiply_fusion = f32[27,192,96]{2,1,0:T(8,128)} fusion(bf16[27,192,96]{2,1,0:T(8,128)(2,1)S(1)} %get-tuple-element.11), kind=kLoop, calls=%fused_computation | loop fusion | flops 995328 | bytes 2985984 | tf_op jit(solution)/shard_map/mul | solution.py:585
  64.5 1.2 %convert_multiply_fusion.1 = f32[27,96,96]{2,1,0:T(8,128)} fusion(bf16[27,96,96]{2,1,0:T(8,128)(2,1)S(1)} %get-tuple-element.10), kind=kLoop, calls=%fused_computation.1 | loop fusion | flops 497664 | bytes 1492992 | tf_op jit(solution)/shard_map/mul | solution.py:584
  65.7 1.1 %copy.11 = bf16[1,96,2,4,256]{4,3,2,1,0:T(4,128)(2,1)} copy(bf16[1,96,2,4,256]{4,1,3,2,0:T(8,128)(2,1)S(1)} %bitcast.14) | data formatting | bytes 786432
  66.7 0.6 copy.15
